TPU v7x, 256 devices: a whole 4x4x8 slice. The times are simulated.
256 devices in a mesh: dp: 64 (over z, y_lo, x), tensor: 4 (over y_hi, core).
Axes of the slice: x: 4, y: 4 (y_hi: 2, y_lo: 2; y = y_hi * 2 + y_lo), z: 8, core: 2. Of those that a mesh axis runs over, the one named last changes fastest.
Arguments:
- queries: bfloat16 [32768, 2048], P('dp', 'tensor'), may hold values from -2.5 to 2.5
- keys: bfloat16 [32768, 2048], P('dp', 'tensor'), may hold values from -2.5 to 2.5
- values: bfloat16 [32768, 2048], P('dp', 'tensor'), may hold values from -6 to 6
- attended: bfloat16 [32768, 2048], P('dp', 'tensor'), may hold values from -6 to 6
- upstream: bfloat16 [32768, 4096], P(('dp', 'tensor')), may hold values from -24 to 24
- out_weight: bfloat16 [2048, 4096], P('tensor', 'dp'), may hold values from -0.125 to 0.125
- bias_table: float32 [32, 32], P(None, 'tensor'), may hold values from -4 to 4
- buckets: int32 [511], replicated, may hold values from 0 to 31
- segments: int32 [32768], P('dp'), may hold values from 0 to 2, as said below
Outputs:
- query_grad: bfloat16 [32768, 2048], P('dp', 'tensor')
- key_grad: bfloat16 [32768, 2048], P('dp', 'tensor')
- value_grad: bfloat16 [32768, 2048], P('dp', 'tensor')
- weight_grad: float32 [4096, 2048], P('dp', 'tensor')
- table_grad: float32 [32, 32], P(None, 'tensor')
Inputs may be any that keep to these rules, and one draw needn't show every extreme that they name: `segments`: within each group of 512 rows, ids start at 0 and rise by one at each passage boundary; every passage has at most 256 tokens and the group holds one of exactly 256.
All inputs are finite; a program needn't handle non-finite values.
Results may differ from a plain program's by a relative error of at most 0.0076.
Values may be sent and summed in bfloat16 or wider, within the bound.
A program may use at most 64 MiB of HBM per device.

v0:
```python
import jax
import jax.numpy as jnp
from jax import lax
from jax.sharding import PartitionSpec as P

HDIM = 64
PLEN = 256


def split_heads(block, count):
    return block.reshape(block.shape[0], count, HDIM).transpose(1, 0, 2)


def join_heads(stacked):
    return stacked.transpose(1, 0, 2).reshape(stacked.shape[1], stacked.shape[0] * stacked.shape[2])


def term_maker(grad_full, columns_of):
    return lax.dot_general(
        grad_full, columns_of, (((0,), (0,)), ((), ())), preferred_element_type=jnp.float32
    )


def toeplitz_bias(bias_col, rows_all):
    margin = rows_all - PLEN
    first_val = jnp.broadcast_to(bias_col[0], (margin,))
    last_val = jnp.broadcast_to(bias_col[-1], (margin,))
    extended = jnp.concatenate([first_val, bias_col, last_val])
    padded = jnp.concatenate([extended[::-1], jnp.zeros((1,), jnp.float32)])
    tiled = jnp.broadcast_to(padded[None, :], (rows_all, 2 * rows_all)).reshape(-1)
    skewed = tiled[: rows_all * (2 * rows_all - 1)].reshape(rows_all, 2 * rows_all - 1)
    return skewed[:, rows_all - 1 :]


def offset_sums(dscores, rows_all):
    flipped = dscores[:, ::-1]
    padded = jnp.concatenate(
        [flipped, jnp.zeros((rows_all, rows_all), jnp.float32)], axis=1
    ).reshape(-1)
    skewed = padded[: rows_all * (2 * rows_all - 1)].reshape(rows_all, 2 * rows_all - 1)
    diagonal = jnp.sum(skewed, axis=0)
    margin = rows_all - PLEN
    middle = diagonal[margin : margin + 2 * PLEN - 1]
    low_tail = jnp.sum(diagonal[:margin])
    high_tail = jnp.sum(diagonal[margin + 2 * PLEN - 1 :])
    middle = middle.at[0].add(low_tail)
    middle = middle.at[2 * PLEN - 2].add(high_tail)
    return middle


def on_device(queries, keys, values, attended, upstream, out_weight, bias_table, buckets, segments):
    rows_all = queries.shape[0]
    heads_here = queries.shape[1] // HDIM
    grad_full = lax.all_gather(upstream, "tensor", axis=0, tiled=True)
    weight_full = lax.all_gather(out_weight, "dp", axis=1, tiled=True)
    grad_ctx = lax.dot_general(
        grad_full, weight_full, (((1,), (1,)), ((), ())), preferred_element_type=jnp.float32
    )
    grad_ctx = grad_ctx.astype(jnp.bfloat16)
    weight_grad = lax.psum_scatter(
        term_maker(grad_full, attended), "dp", scatter_dimension=0, tiled=True
    )
    onehot = (buckets[:, None] == jnp.arange(bias_table.shape[0], dtype=jnp.int32)[None, :]).astype(
        jnp.float32
    )
    bias_off = jnp.dot(onehot, bias_table, precision=lax.Precision.HIGHEST)
    same = segments[:, None] == segments[None, :]

    def one_head(items):
        q_head, k_head, v_head, g_head, bias_col = items
        scores = lax.dot_general(
            q_head, k_head, (((1,), (1,)), ((), ())), preferred_element_type=jnp.float32
        )
        scores = scores + toeplitz_bias(bias_col, rows_all)
        scores = jnp.where(same, scores, -jnp.inf)
        peak = jnp.max(scores, axis=1, keepdims=True)
        expd = jnp.exp(scores - peak)
        probs = expd / jnp.sum(expd, axis=1, keepdims=True)
        probs_b = probs.astype(jnp.bfloat16)
        dprobs = lax.dot_general(
            g_head, v_head, (((1,), (1,)), ((), ())), preferred_element_type=jnp.float32
        )
        delta = jnp.sum(probs * dprobs, axis=1, keepdims=True)
        dscores = probs * (dprobs - delta)
        ds_b = dscores.astype(jnp.bfloat16)
        q_grad = jnp.dot(ds_b, k_head, preferred_element_type=jnp.float32).astype(jnp.bfloat16)
        k_grad = lax.dot_general(
            ds_b, q_head, (((0,), (0,)), ((), ())), preferred_element_type=jnp.float32
        ).astype(jnp.bfloat16)
        v_grad = lax.dot_general(
            probs_b, g_head, (((0,), (0,)), ((), ())), preferred_element_type=jnp.float32
        ).astype(jnp.bfloat16)
        off_grad = offset_sums(dscores, rows_all)
        return (q_grad, k_grad, v_grad, off_grad)

    stacked = (
        split_heads(queries, heads_here),
        split_heads(keys, heads_here),
        split_heads(values, heads_here),
        split_heads(grad_ctx, heads_here),
        bias_off.T,
    )
    q_grad, k_grad, v_grad, off_grad = lax.map(one_head, stacked)
    table_local = jnp.dot(onehot.T, off_grad.T, precision=lax.Precision.HIGHEST)
    table_grad = lax.psum(table_local, "dp")
    return (join_heads(q_grad), join_heads(k_grad), join_heads(v_grad), weight_grad, table_grad)


def solution(mesh):
    in_specs = (
        P("dp", "tensor"),
        P("dp", "tensor"),
        P("dp", "tensor"),
        P("dp", "tensor"),
        P(("dp", "tensor"), None),
        P("tensor", "dp"),
        P(None, "tensor"),
        P(),
        P("dp"),
    )
    out_specs = (
        P("dp", "tensor"),
        P("dp", "tensor"),
        P("dp", "tensor"),
        P("dp", "tensor"),
        P(None, "tensor"),
    )
    return jax.shard_map(
        on_device, mesh=mesh, in_specs=in_specs, out_specs=out_specs, check_vma=False
    )
```

profile of v0, /device:TPU:16, one launch (start us, length us, event | category | flops | bytes accessed | tf_op | source)
XLA Modules:
  0.0 732.2 jit_solution(18144987541202989379)
XLA Ops:
  10.0 2.0 copy.33
  12.1 2.0 copy.35
  14.4 36.6 %all-gather.3.cloned.1.call-done = bf16[512,4096]{1,0:T(8,128)(2,1)} async-done(((bf16[128,4096]{1,0:T(8,128)(2,1)}), bf16[512,4096]{1,0:T(8,128)(2,1)}) %all-gather.3.cloned.1.call-update) | async-done | bytes 4194320 | tf_op jit(solution)/shard_map/all_gather | solution.py:54
  51.0 7.8 %fusion.39 = f32[4096,512]{1,0:T(8,128)} fusion(bf16[512,4096]{1,0:T(8,128)(2,1)} %all-gather.3.cloned.1.call-done, bf16[512,512]{1,0:T(8,128)(2,1)S(1)} %copy-done), kind=kOutput, calls=%fused_computation.56 | convolution fusion | flops 2147483648 | bytes 13107200 | tf_op jit(solution)/shard_map/dot_general | solution.py:19
  58.9 299.5 %all-gather.5.cloned.1.call-done = bf16[512,4096]{0,1:T(8,128)(2,1)} async-done(((bf16[512,64]{0,1:T(8,128)(2,1)}), bf16[512,4096]{0,1:T(8,128)(2,1)}) %all-gather.5.cloned.1.call-update) | async-done | bytes 4194320 | tf_op jit(solution)/shard_map/all_gather | solution.py:55
  358.4 5.8 convolution_convert_fusion.3
  365.6 196.2 %while.22 = (s32[]{:T(128)}, bf16[8,512,64]{1,2,0:T(8,128)(2,1)}, bf16[8,512,64]{1,2,0:T(8,128)(2,1)}, bf16[8,512,64]{1,2,0:T(8,128)(2,1)}, f32[8,511]{1,0:T(8,1...) while((s32[]{:T(128)}, bf16[8,512,64]{1,2,0:T(8,128)(2,1)}, ...), condition=%wide.region_7.8_spmd.clone, body=%wide.region_0.7_spmd.clone.sunk | while | flops 173376000 | bytes 44906716 | solution.py:103
  368.4 2.8 reshape.154
  381.8 1.9 copy.56
  383.6 3.0 reshape.155
  393.0 2.8 reshape.154
  406.3 1.9 copy.56
  408.2 3.0 reshape.155
  417.5 2.8 reshape.154
  430.8 1.9 copy.56
  432.7 3.0 reshape.155
  442.0 2.8 reshape.154
  455.4 1.9 copy.56
  457.2 3.0 reshape.155
  466.5 2.8 reshape.154
  479.9 1.9 copy.56
  481.8 3.0 reshape.155
  491.1 2.8 reshape.154
  506.3 3.0 reshape.155
  515.6 2.8 reshape.154
  530.8 3.0 reshape.155
  540.1 2.8 reshape.154
  555.4 3.0 reshape.155
  561.8 2.0 copy.39
  563.8 2.0 copy.40
  565.9 2.0 copy.41
  568.2 157.4 %psum.7 = f32[32,8]{0,1:T(8,128)} all-reduce(f32[32,8]{0,1:T(8,128)S(1)} %fusion.35), channel_id=1, replica_groups=mesh['dp'=64,'tensor'=4] {'dp'}, use_global_device_ids=true, to_apply=%region_9.10 | all-reduce | flops 256 | bytes 2048 | tf_op jit(solution)/shard_map/psum | solution.py:105
  (258 shorter events, 134.5 us)
Async XLA Ops:
  7.2 43.9 %copy-start = (bf16[512,512]{1,0:T(8,128)(2,1)S(1)}, bf16[512,512]{1,0:T(8,128)(2,1)}, u32[]{:S(2)}) copy-start(bf16[512,512]{1,0:T(8,128)(2,1)} %param.18) | copy-start | bytes 1572868
  7.2 6.9 copy-start.3
  7.2 6.9 copy-start.2
  7.2 43.8 %all-gather.3.cloned.1.call-start = ((), (), s32[]{:S(2)}) async-start(), calls=%async_computation.1 | async-start | bytes 5242880 | tf_op jit(solution)/shard_map/all_gather | solution.py:54
  7.9 350.5 %all-gather.5.cloned.1.call-start = ((), (), s32[]{:S(2)}) async-start(), calls=%async_computation.2 | async-start | bytes 4259840 | tf_op jit(solution)/shard_map/all_gather | solution.py:55
  8.7 717.0 %reduce-scatter.2.cloned.1.call-start = ((), (), s32[]{:S(2)}) async-start(), calls=%async_computation.3 | async-start | bytes 8519680 | tf_op jit(solution)/shard_map/reduce_scatter | solution.py:60
  58.9 306.7 %copy-start.1 = (s32[512]{0:T(512)S(1)}, s32[512]{0:T(512)}, u32[]{:S(2)}) copy-start(s32[512]{0:T(512)} %param.23) | copy-start | bytes 6148
Sparse Core Ops, SparseCore 0:
  9.8 41.1 all-gather.2
  52.8 305.5 all-gather.4
  361.5 329.4 reduce-scatter.1
where the time goes:
time: 734 us; the launch traced here: 732 us
  waiting for transfers between devices  338 us (46%)
  blocking collectives  157 us (21%)
  local copies, waits for them, and re-layouts  126 us (17%)
  matrix products  69.6 us (9%)
  other arithmetic  16.8 us (2%)
  between operations  13.8 us (2%)
  loops' own time  10.6 us (1%)
    all_gather x1, waiting for transfers between devices, on_device(): weight_full = lax.all_gather(out_weight, 'dp', axis=1, tiled=True)  300 us
    psum x1, blocking collectives, on_device(): table_grad = lax.psum(table_local, 'dp')  157 us
    all_gather x1, waiting for transfers between devices, on_device(): grad_full = lax.all_gather(upstream, 'tensor', axis=0, tiled=True)  36.6 us
    while x64, local copies, waits for them, and re-layouts  29.1 us
    reshape x8, local copies, waits for them, and re-layouts, offset_sums(): padded[:rows_all * (2 * rows_all - 1)].reshape(rows_all, 2 * rows_all - 1)  23.8 us
    reshape x8, local copies, waits for them, and re-layouts, toeplitz_bias(): tiled[:rows_all * (2 * rows_all - 1)].reshape(rows_all, 2 * rows_all - 1)  22.7 us
    dot_general x8, matrix products, one_head(): lax.dot_general(probs_b, g_head, (((0,), (0,)), ((), ())), preferred_elem...  14.8 us
  transfers between devices with their start and end apart: 3, of which 2 were waited for; matrix products, arithmetic and copies ran while one was open for 29% of the time, Pallas kernels for 0%

commit v1 on v0

v1 whole, which is shorter than its diff:
```python
import functools

import jax
import jax.numpy as jnp
from jax import lax
from jax.experimental import pallas as pl
from jax.experimental.pallas import tpu as pltpu
from jax.sharding import PartitionSpec as P

MESH = pl.DeviceIdType.MESH
F32 = jnp.float32
BF16 = jnp.bfloat16
ROWS = 512
FEAT = 512
HALF = 256
D = 4096
HEADS = 8
WIDE = 768
BLOCK = 128
FAR = -4096.0
N_SEM = 96


def nt(a, b):
    return lax.dot_general(a, b, (((1,), (1,)), ((), ())), preferred_element_type=F32)


def nn(a, b):
    return jnp.dot(a, b, preferred_element_type=F32)


class Wire:
    def __init__(self, send_sem, recv_sem):
        self.send_sem, self.recv_sem = send_sem, recv_sem
        self.made = []

    def send(self, src, dst, device):
        at = len(self.made)
        copy = pltpu.make_async_remote_copy(
            src_ref=src,
            dst_ref=dst,
            send_sem=self.send_sem.at[at],
            recv_sem=self.recv_sem.at[at],
            device_id=device,
            device_id_type=MESH,
        )
        copy.start()
        self.made.append(copy)
        return copy

    def finish(self):
        for copy in self.made:
            copy.wait_send()


def kernel(
    q_hbm, k_hbm, v_hbm, att_hbm, up_hbm, wt_hbm, table_ref, bucket_ref, seg_ref,
    dq_ref, dk_ref, dv_ref, wg_ref, tg_ref,
    q_ref, k_ref, v_ref, att_ref, g_ref, ctx_ref, wa_ref, wb_ref, fp_ref, fm_ref,
    ta_ref, tb_ref, rap_ref, ram_ref, sa_ref, saf_ref, rax_ref, ray_ref, say_ref,
    rbp_ref, rbm_ref, sby_ref, sbf_ref, rby_ref, sbz_ref, rbz_ref,
    e_ref, r_ref, dp_ref, pb_ref, dsb_ref, toe_ref, bext_ref, oh_ref, gb_ref, g8_ref,
    qaug_ref, kaug_ref, dqt_ref, dkp_ref, dvp_ref,
    tz_ref, rtz_ref, tx_ref, rtx_ref, ty_ref, rty_ref,
    local_sem, send_sem, recv_sem,
):
    me, tensor = lax.axis_index("dp"), lax.axis_index("tensor")
    x, yl, z = lax.rem(me, 4), lax.rem(lax.div(me, 4), 2), lax.div(me, 8)
    core, yh = lax.rem(tensor, 2), lax.div(tensor, 2)
    y = yh * 2 + yl

    def place(z_at, yl_at, x_at, yh_at, core_at):
        return {"dp": z_at * 8 + yl_at * 4 + x_at, "tensor": yh_at * 2 + core_at}

    def xs(k):
        return lax.rem(x + k, 4)

    def zs(k):
        return lax.rem(z + k, 8)

    def at_x(k):
        return place(z, yl, xs(k), yh, core)

    def at_z(k):
        return place(zs(k), yl, x, yh, core)

    def at_y(k):
        there = lax.rem(y + k, 4)
        return place(z, lax.rem(there, 2), x, lax.div(there, 2), core)

    pair = place(z, 1 - yl, x, yh, core)
    mate = place(z, yl, x, yh, 1 - core)

    loads = []
    for at, (src, dst) in enumerate(
        [
            (q_hbm, q_ref),
            (k_hbm, k_ref),
            (v_hbm, v_ref),
            (att_hbm, att_ref),
            (up_hbm, g_ref.at[pl.ds(pl.multiple_of(tensor * 128, 128), 128), :]),
            (wt_hbm.at[:, pl.ds(0, HALF)], wa_ref.at[z, yl, x]),
            (wt_hbm.at[:, pl.ds(HALF, HALF)], wb_ref.at[z, yl, x]),
        ]
    ):
        copy = pltpu.make_async_copy(src, dst, local_sem.at[at])
        copy.start()
        loads.append(copy)

    barrier = pltpu.get_barrier_semaphore()
    greeted = [at_z(k) for k in range(1, 8)] + [at_x(k) for k in range(1, 4)] + [at_y(1), at_y(3), mate]
    for device in greeted:
        pl.semaphore_signal(barrier, inc=1, device_id=device, device_id_type=MESH)
    pl.semaphore_wait(barrier, len(greeted))

    wire = Wire(send_sem, recv_sem)

    y_pair = wire.send(wt_hbm.at[:, pl.ds(0, HALF)], wa_ref.at[z, yl, x], pair)
    b_z = [
        wire.send(wt_hbm.at[:, pl.ds(HALF, HALF)], wb_ref.at[z, yl, x], at_z(k)) for k in range(1, 8)
    ]
    own_rows = pl.multiple_of(tensor * 128, 128)
    up_fp, up_fm = [], []
    for c in range(2):
        up_fp.append(wire.send(up_hbm.at[pl.ds(c * 32, 32), :], fp_ref.at[c], at_y(1)))
        up_fm.append(wire.send(up_hbm.at[pl.ds(64 + c * 32, 32), :], fm_ref.at[c], at_y(3)))
    to_mate = [wire.send(up_hbm, g_ref.at[pl.ds(own_rows, 128), :], mate)]
    for copy in loads:
        copy.wait()

    before = lax.div(lax.rem(y + 3, 4), 2) * 2 + core
    after = lax.div(lax.rem(y + 1, 4), 2) * 2 + core
    across = (1 - yh) * 2 + core
    got = {}

    def gather_a2():
        y_pair.wait_recv()
        got["a_x"] = [wire.send(wa_ref.at[z, :, x], wa_ref.at[z, :, x], at_x(k)) for k in (1, 3, 2)]

    def a_hop(step, way, part):
        chunk = wa_ref.at[zs(8 - (step - 1) if way == 1 else step - 1), part]
        return wire.send(chunk, chunk, at_z(1 if way == 1 else 7))

    def gather_a3():
        for copy in got["a_x"]:
            copy.wait_recv()
        for part in range(2):
            for way in (1, -1):
                got["a_z", 1, way, part] = a_hop(1, way, part)

    def gather_a_step(step):
        for part in range(2):
            for way in (1, -1):
                got["a_z", step, way, part].wait_recv()
                if step < 3 or (part == 0) == (way == 1):
                    got["a_z", step + 1, way, part] = a_hop(step + 1, way, part)

    def gather_a_end():
        got["a_z", 4, 1, 0].wait_recv()
        got["a_z", 4, -1, 1].wait_recv()

    def gather_b2():
        for copy in b_z:
            copy.wait_recv()
        got["b_y"] = wire.send(wb_ref.at[:, yl, x], wb_ref.at[:, yl, x], pair)

    def gather_b3():
        got["b_y"].wait_recv()
        for part in range(2):
            chunk = wb_ref.at[pl.ds(part * 4, 4), :, x]
            for way in (1, 3):
                got["b_x", 1, way, part] = wire.send(chunk, chunk, at_x(way))

    def gather_b4(part):
        for way in (1, 3):
            got["b_x", 1, way, part].wait_recv()
        way = 1 if part == 0 else 3
        chunk = wb_ref.at[pl.ds(part * 4, 4), :, xs(3 if part == 0 else 1)]
        got["b_x", 2, part] = wire.send(chunk, chunk, at_x(way))

    def gather_b_end():
        for part in range(2):
            got["b_x", 2, part].wait_recv()

    def rows_of(owner, first, count):
        return g_ref.at[pl.ds(pl.multiple_of(owner * 128 + first, 32), count), :]

    def up_hand_on(c):
        up_fp[c].wait_recv()
        got["u", 0, c] = wire.send(fp_ref.at[c], rows_of(before, c * 32, 32), at_y(1))
        up_fm[c].wait_recv()
        got["u", 1, c] = wire.send(fm_ref.at[c], rows_of(after, 64 + c * 32, 32), at_y(3))

    def up_share(c):
        for side in range(2):
            got["u", side, c].wait_recv()
            block = rows_of(across, side * 64 + c * 32, 32)
            to_mate.append(wire.send(block, block, mate))

    def up_end():
        for copy in to_mate:
            copy.wait_recv()

    def prepare():
        lane = lax.broadcasted_iota(jnp.int32, (ROWS, BLOCK), 1)
        spot = jnp.where(lane < 64, lane, lane - 64)
        seg = jnp.broadcast_to(seg_ref[...].astype(F32), (BLOCK, ROWS)).T
        same = seg == spot.astype(F32)
        qaug_ref[...] = jnp.where(same, 1.0, 0.0).astype(BF16)
        kaug_ref[...] = jnp.where((spot < 3) & jnp.logical_not(same), FAR, 0.0).astype(BF16)
        oh_ref[...] = jnp.where(
            lax.broadcasted_iota(jnp.int32, (32, WIDE), 0) == bucket_ref[...], 1.0, 0.0
        )
        bext_ref[...] = jnp.dot(
            table_ref[...], oh_ref[...], precision=lax.Precision.HIGHEST, preferred_element_type=F32
        )
        pb_ref[...] = jnp.zeros_like(pb_ref)
        dsb_ref[...] = jnp.zeros_like(dsb_ref)

    def columns(p):
        return pl.ds(pl.multiple_of(p * BLOCK, BLOCK), BLOCK)

    def own_lanes(odd):
        lane = lax.broadcasted_iota(jnp.int32, (ROWS, BLOCK), 1)
        return (lane >= 64) if odd else (lane < 64)

    def softmax_pair(p):
        qp, kp = q_ref[:, columns(p)], k_ref[:, columns(p)]
        for odd in range(2):
            h = 2 * p + odd
            own = own_lanes(odd)
            q_h = jnp.where(own, qp, qaug_ref[...])
            k_h = jnp.where(own, kp, kaug_ref[...])
            bias = bext_ref[pl.ds(h, 1), :]
            for d in range(5):
                strip = jnp.broadcast_to(bias[:, d * BLOCK : (d + 2) * BLOCK], (BLOCK, 2 * BLOCK))
                toe_ref[d] = pltpu.roll(strip, 0, 1, stride=1, stride_axis=0)[:, BLOCK:]
            for i2 in range(2):
                peak = [None, None]
                for j in range(4):
                    s2 = nt(k_h[j * BLOCK : (j + 1) * BLOCK], q_h[i2 * 256 : (i2 + 1) * 256])
                    for sub in range(2):
                        i = 2 * i2 + sub
                        if abs(i - j) <= 2:
                            s = s2[:, sub * BLOCK : (sub + 1) * BLOCK] + toe_ref[i - j + 2]
                            e_ref[h, j * BLOCK : (j + 1) * BLOCK, i * BLOCK : (i + 1) * BLOCK] = s
                            top = jnp.max(s.reshape(16, 8, BLOCK), axis=0)
                            peak[sub] = top if peak[sub] is None else jnp.maximum(peak[sub], top)
                for sub in range(2):
                    i = 2 * i2 + sub
                    top = jnp.max(peak[sub], axis=0, keepdims=True)
                    total = None
                    for j in range(4):
                        if abs(i - j) <= 2:
                            at = (h, slice(j * BLOCK, (j + 1) * BLOCK), slice(i * BLOCK, (i + 1) * BLOCK))
                            e = jnp.exp(e_ref[at] - top)
                            e_ref[at] = e
                            part = jnp.sum(e.reshape(16, 8, BLOCK), axis=0)
                            total = part if total is None else total + part
                    r_ref[pl.ds(h, 1), i * BLOCK : (i + 1) * BLOCK] = 1.0 / jnp.sum(
                        total, axis=0, keepdims=True
                    )

    def context(which, m):
        w = (wa_ref if which == 0 else wb_ref)[...].reshape(D, HALF)
        rows = slice(m * 256, (m + 1) * 256)
        ctx_ref[rows, which * HALF : (which + 1) * HALF] = nn(g_ref[rows, :], w).astype(BF16)

    def backward_pair(p):
        qp, kp = q_ref[:, columns(p)], k_ref[:, columns(p)]
        vp, gp = v_ref[:, columns(p)], ctx_ref[:, columns(p)]
        kpt = kp.T
        for odd in range(2):
            h = 2 * p + odd
            own = own_lanes(odd)
            g_h = jnp.where(own, gp, jnp.zeros_like(gp))
            delta = []
            for i2 in range(2):
                sums = [None, None]
                for j in range(4):
                    d2 = nt(vp[j * BLOCK : (j + 1) * BLOCK], g_h[i2 * 256 : (i2 + 1) * 256])
                    for sub in range(2):
                        i = 2 * i2 + sub
                        if abs(i - j) <= 2:
                            js, cs = slice(j * BLOCK, (j + 1) * BLOCK), slice(i * BLOCK, (i + 1) * BLOCK)
                            d1 = d2[:, sub * BLOCK : (sub + 1) * BLOCK]
                            dp_ref[js, cs] = d1
                            part = jnp.sum((e_ref[h, js, cs] * d1).reshape(16, 8, BLOCK), axis=0)
                            sums[sub] = part if sums[sub] is None else sums[sub] + part
                for sub in range(2):
                    i = 2 * i2 + sub
                    recip = r_ref[pl.ds(h, 1), i * BLOCK : (i + 1) * BLOCK]
                    delta.append(recip * jnp.sum(sums[sub], axis=0, keepdims=True))
            g8_ref[...] = jnp.zeros_like(g8_ref)
            for d in range(-2, 3):
                diag = None
                for j in range(4):
                    i = j + d
                    if 0 <= i < 4:
                        js, cs = slice(j * BLOCK, (j + 1) * BLOCK), slice(i * BLOCK, (i + 1) * BLOCK)
                        probs = e_ref[h, js, cs] * r_ref[pl.ds(h, 1), cs]
                        ds = probs * (dp_ref[js, cs] - delta[i])
                        pb_ref[js, cs] = probs.astype(BF16)
                        dsb_ref[js, cs] = ds.astype(BF16)
                        diag = ds if diag is None else diag + ds
                strip = jnp.concatenate([jnp.zeros_like(diag), diag], axis=1)
                total = strip[0:8]
                for g in range(1, 16):
                    total = total + pltpu.roll(strip[8 * g : 8 * g + 8], 2 * BLOCK - 8 * g, 1)
                cs = slice((d + 2) * BLOCK, (d + 4) * BLOCK)
                g8_ref[:, cs] = g8_ref[:, cs] + total
            row = g8_ref[0:1, :]
            for s in range(1, 8):
                row = row + pltpu.roll(g8_ref[s : s + 1, :], WIDE - s, 1)
            gb_ref[pl.ds(h, 1), :] = row
            side = slice(64 * odd, 64 * odd + 64)
            dqt_ref[side, :] = nn(kpt[side, :], dsb_ref[...])
            dk_h, dv_h = nn(dsb_ref[...], qp), nn(pb_ref[...], gp)
            if odd == 0:
                dkp_ref[...] = dk_h
                dvp_ref[...] = dv_h
            else:
                dk_ref[:, columns(p)] = jnp.where(own, dk_h, dkp_ref[...]).astype(BF16)
                dv_ref[:, columns(p)] = jnp.where(own, dv_h, dvp_ref[...]).astype(BF16)
        dq_ref[:, columns(p)] = dqt_ref[...].T.astype(BF16)

    def term(k):
        z_at = zs(k)
        block = lax.dot_general(
            g_ref[:, pl.ds(pl.multiple_of(z_at * 512, 512), 512)],
            att_ref[...],
            (((0,), (0,)), ((), ())),
            preferred_element_type=F32,
        ).astype(BF16)
        ta_ref[z_at] = block[:, :HALF].reshape(2, 4, 64, HALF)
        tb_ref[z_at] = block[:, HALF:].reshape(2, 4, 64, HALF)

    def sum_a_hop(k, way, part):
        come = rap_ref if way == 1 else ram_ref
        z_at = zs(k if way == 1 else 8 - k)
        if ("sa", k, way, part) in got:
            got["sa", k, way, part].wait_recv()
            ta_ref[z_at, part] = (
                ta_ref[z_at, part].astype(F32) + come[k, part].astype(F32)
            ).astype(BF16)
        got["sa", k - 1, way, part] = wire.send(
            ta_ref.at[z_at, part], come.at[k - 1, part], at_z(1 if way == 1 else 7)
        )

    def sum_a_step(k):
        for part in range(2):
            for way in (1, -1):
                if k < 4 or (part == 0) == (way == 1):
                    sum_a_hop(k, way, part)

    def sum_a_x():
        for part in range(2):
            for way in (1, -1):
                got["sa", 0, way, part].wait_recv()
            full = (
                ta_ref[z, part].astype(F32) + rap_ref[0, part].astype(F32) + ram_ref[0, part].astype(F32)
            )
            saf_ref[part] = full
            sa_ref[part] = full.astype(BF16)
        for k in (1, 3, 2):
            got["sax", k] = wire.send(sa_ref.at[:, xs(k)], rax_ref.at[k - 1], at_x(k))

    def sum_a_y():
        full = saf_ref[:, x]
        for k in (1, 3, 2):
            got["sax", k].wait_recv()
            full = full + rax_ref[k - 1].astype(F32)
        saf_ref[:, x] = full
        say_ref[...] = full.astype(BF16)
        got["say"] = wire.send(say_ref.at[1 - yl], ray_ref, pair)

    def sum_a_end():
        got["say"].wait_recv()
        wg_ref[:, :HALF] = saf_ref[yl, x] + ray_ref[...].astype(F32)

    def part_b(part):
        return pl.ds(part * 4, 4)

    def sum_b_first():
        got["sb", 1, 1, 0] = wire.send(tb_ref.at[part_b(0), :, xs(2)], rbp_ref.at[1], at_x(1))
        got["sb", 1, 3, 1] = wire.send(tb_ref.at[part_b(1), :, xs(2)], rbm_ref.at[1], at_x(3))
        sum_b_hop(1, 1)
        sum_b_hop(3, 0)

    def sum_b_hop(way, part):
        come = rbp_ref if way == 1 else rbm_ref
        if ("sb", 1, way, part) in got:
            got["sb", 1, way, part].wait_recv()
            at = (part_b(part), slice(None), xs(way))
            tb_ref[at] = (tb_ref[at].astype(F32) + come[1].astype(F32)).astype(BF16)
        got["sb", 0, way, part] = wire.send(
            tb_ref.at[part_b(part), :, xs(way)],
            (come.at[0] if (part == 0) == (way == 1) else come.at[2]),
            at_x(way),
        )

    def sum_b_second():
        sum_b_hop(1, 0)
        sum_b_hop(3, 1)

    def sum_b_y():
        for part in (1, 0):
            for way in (1, 3):
                got["sb", 0, way, part].wait_recv()
        for part in range(2):
            up = rbp_ref[0 if part == 0 else 2].astype(F32)
            down = rbm_ref[2 if part == 0 else 0].astype(F32)
            full = tb_ref[part_b(part), :, x].astype(F32) + up + down
            sbf_ref[part_b(part)] = full
            sby_ref[part_b(part)] = full.astype(BF16)
        got["sby"] = wire.send(sby_ref.at[:, 1 - yl], rby_ref, pair)

    def sum_b_z():
        got["sby"].wait_recv()
        full = sbf_ref[:, yl] + rby_ref[...].astype(F32)
        sbf_ref[:, 0] = full
        sbz_ref[...] = full.astype(BF16)
        for k in range(1, 8):
            got["sbz", k] = wire.send(sbz_ref.at[zs(k)], rbz_ref.at[k - 1], at_z(k))

    def sum_b_end():
        full = sbf_ref[z, 0]
        for k in range(1, 8):
            got["sbz", k].wait_recv()
            full = full + rbz_ref[k - 1].astype(F32)
        wg_ref[:, HALF:] = full

    def table_z():
        here = lax.dot_general(
            gb_ref[...], oh_ref[...], (((1,), (1,)), ((), ())),
            precision=lax.Precision.HIGHEST, preferred_element_type=F32,
        )
        tz_ref[...] = jnp.concatenate([here, jnp.zeros((HEADS, BLOCK - 32), F32)], axis=1)
        for k in range(1, 8):
            got["tz", k] = wire.send(tz_ref, rtz_ref.at[k - 1], at_z(k))

    def table_x():
        full = tz_ref[...]
        for k in range(1, 8):
            got["tz", k].wait_recv()
            full = full + rtz_ref[k - 1]
        tx_ref[...] = full
        for k in range(1, 4):
            got["tx", k] = wire.send(tx_ref, rtx_ref.at[k - 1], at_x(k))

    def table_y():
        full = tx_ref[...]
        for k in range(1, 4):
            got["tx", k].wait_recv()
            full = full + rtx_ref[k - 1]
        ty_ref[...] = full
        got["ty"] = wire.send(ty_ref, rty_ref, pair)

    def table_end():
        got["ty"].wait_recv()
        tg_ref[...] = (ty_ref[...] + rty_ref[...])[:, :32]

    prepare()
    gather_a2()
    gather_a3()
    gather_b2()
    softmax_pair(0)
    up_hand_on(0)
    gather_a_step(1)
    gather_b3()
    up_hand_on(1)
    softmax_pair(1)
    gather_a_step(2)
    up_share(0)
    softmax_pair(2)
    gather_b4(0)
    gather_a_step(3)
    gather_b4(1)
    up_share(1)
    softmax_pair(3)
    up_end()
    for k in (4, 3, 5):
        term(k)
        if k == 4:
            sum_a_step(4)
    for part in range(2):
        for way in (1, -1):
            if ("sa", 3, way, part) not in got:
                sum_a_hop(3, way, part)
    for k in (2, 6, 1, 7, 0):
        term(k)
    sum_b_first()
    for part, way in ((0, 1), (1, -1)):
        sum_a_hop(3, way, part)
    gather_a_end()
    context(0, 0)
    context(0, 1)
    gather_b_end()
    sum_a_step(2)
    context(1, 0)
    context(1, 1)
    sum_b_second()
    backward_pair(0)
    sum_a_step(1)
    backward_pair(1)
    sum_b_y()
    sum_a_x()
    backward_pair(2)
    sum_b_z()
    sum_a_y()
    backward_pair(3)
    table_z()
    sum_a_end()
    table_x()
    sum_b_end()
    table_y()
    table_end()
    wire.finish()


def on_device(queries, keys, values, attended, upstream, out_weight, bias_table, buckets, segments):
    shifted = jnp.pad(buckets, (129, WIDE - 129 - buckets.shape[0]), constant_values=-1)[None, :]
    anywhere = pl.BlockSpec(memory_space=pl.ANY)
    inside = pl.BlockSpec(memory_space=pltpu.VMEM)
    bf, f4 = (lambda *s: pltpu.VMEM(s, BF16)), (lambda *s: pltpu.VMEM(s, F32))
    dq, dk, dv, wg, tg = pl.pallas_call(
        kernel,
        out_shape=(
            jax.ShapeDtypeStruct((ROWS, FEAT), BF16),
            jax.ShapeDtypeStruct((ROWS, FEAT), BF16),
            jax.ShapeDtypeStruct((ROWS, FEAT), BF16),
            jax.ShapeDtypeStruct((64, FEAT), F32),
            jax.ShapeDtypeStruct((HEADS, 32), F32),
        ),
        in_specs=[anywhere] * 6 + [inside] * 3,
        out_specs=(inside,) * 5,
        scratch_shapes=[
            bf(ROWS, FEAT), bf(ROWS, FEAT), bf(ROWS, FEAT), bf(ROWS, FEAT),
            bf(ROWS, D), bf(ROWS, FEAT),
            bf(8, 2, 4, 64, HALF), bf(8, 2, 4, 64, HALF),
            bf(2, 32, D), bf(2, 32, D),
            bf(8, 2, 4, 64, HALF), bf(8, 2, 4, 64, HALF),
            bf(4, 2, 4, 64, HALF), bf(4, 2, 4, 64, HALF),
            bf(2, 4, 64, HALF), f4(2, 4, 64, HALF), bf(3, 2, 64, HALF), bf(64, HALF), bf(2, 64, HALF),
            bf(3, 4, 2, 64, HALF), bf(3, 4, 2, 64, HALF),
            bf(8, 2, 64, HALF), f4(8, 2, 64, HALF), bf(8, 64, HALF), bf(8, 64, HALF), bf(7, 64, HALF),
            f4(HEADS, ROWS, ROWS), f4(HEADS, ROWS), f4(ROWS, ROWS), bf(ROWS, ROWS), bf(ROWS, ROWS),
            f4(5, BLOCK, BLOCK), f4(HEADS, WIDE), f4(32, WIDE), f4(HEADS, WIDE), f4(8, WIDE),
            bf(ROWS, BLOCK), bf(ROWS, BLOCK), f4(BLOCK, ROWS), f4(ROWS, BLOCK), f4(ROWS, BLOCK),
            f4(HEADS, BLOCK), f4(7, HEADS, BLOCK), f4(HEADS, BLOCK), f4(3, HEADS, BLOCK),
            f4(HEADS, BLOCK), f4(HEADS, BLOCK),
            pltpu.SemaphoreType.DMA((7,)),
            pltpu.SemaphoreType.DMA((N_SEM,)),
            pltpu.SemaphoreType.DMA((N_SEM,)),
        ],
        compiler_params=pltpu.CompilerParams(
            collective_id=0, has_side_effects=True, vmem_limit_bytes=60 * 1024 * 1024
        ),
    )(
        queries, keys, values, attended, upstream, out_weight.T, bias_table.T, shifted, segments[None, :]
    )
    return dq, dk, dv, wg, tg.T


def solution(mesh):
    in_specs = (
        P("dp", "tensor"),
        P("dp", "tensor"),
        P("dp", "tensor"),
        P("dp", "tensor"),
        P(("dp", "tensor"), None),
        P("tensor", "dp"),
        P(None, "tensor"),
        P(),
        P("dp"),
    )
    out_specs = (
        P("dp", "tensor"),
        P("dp", "tensor"),
        P("dp", "tensor"),
        P("dp", "tensor"),
        P(None, "tensor"),
    )
    return jax.shard_map(
        on_device, mesh=mesh, in_specs=in_specs, out_specs=out_specs, check_vma=False
    )
```

time: 734 us -> 100 us (0.14)
  waiting for transfers between devices: 338 us -> 0 us
  blocking collectives: 157 us -> 0 us
  local copies, waits for them, and re-layouts: 126 us -> 6.79 us
  Pallas kernels: 0 us -> 92.6 us
  matrix products: 69.6 us -> 0 us
  other arithmetic: 16.8 us -> 0 us
  between operations: 13.8 us -> 0.66 us
  loops' own time: 10.6 us -> 0 us
    all_gather x2 -> x0, waiting for transfers between devices: 336 us -> none  [the longest x1 300 us: on_device(): weight_full = lax.all_gather(out_weight, 'dp', axis=1, tiled=True)]
    psum x1 -> x0, blocking collectives: 157 us -> none  [on_device(): table_grad = lax.psum(table_local, 'dp')]
    pallas_call x0 -> x1, Pallas kernels: none -> 92.6 us  [on_device(): pl.pallas_call(kernel, out_shape=(jax.ShapeDtypeStruct((ROWS, FEAT), BF16...]
    dot_general x44 -> x0, matrix products: 69.6 us -> none  [the longest x8 14.8 us: one_head(): lax.dot_general(probs_b, g_head, (((0,), (0,)), ((), ())), preferred_elem...]
    reshape x17 -> x0, local copies, waits for them, and re-layouts: 47.8 us -> none  [the longest x8 23.8 us: offset_sums(): padded[:rows_all * (2 * rows_all - 1)].reshape(rows_all, 2 * rows_all - 1)]
    while x64 -> x0, local copies, waits for them, and re-layouts: 29.1 us -> none
    slice x24 -> x0, local copies, waits for them, and re-layouts: 18.1 us -> none  [the longest x8 13.2 us: toeplitz_bias(): return skewed[:, rows_all - 1:]]
    another operation x1 -> x0, loops' own time: 10.6 us -> none  [on_device(): q_grad, k_grad, v_grad, off_grad = lax.map(one_head, stacked)]
  transfers between devices with their start and end apart: 3 -> 0, of which waited for: 2 -> 0; matrix products, arithmetic and copies ran while one was open for 29% -> 0% of each run, Pallas kernels for 0% -> 0%
where the time goes in v1:
time: 100 us
  Pallas kernels  92.6 us (93%)
  local copies, waits for them, and re-layouts  6.79 us (7%)
    pallas_call x1, Pallas kernels, on_device(): pl.pallas_call(kernel, out_shape=(jax.ShapeDtypeStruct((ROWS, FEAT), BF16...  92.6 us
    unnamed x15, local copies, waits for them, and re-layouts  6.13 us

profile of v1, /device:TPU:16, one launch (start us, length us, event | category | flops | bytes accessed | tf_op | source)
XLA Modules:
  0.0 100.1 jit_solution(2851512884456460654)
XLA Ops:
  0.6 0.0 copy-start.4
  0.6 0.7 copy-done.4
  1.3 0.1 pad.4
  1.4 0.6 broadcast_in_dim.6.bucket_ref
  2.0 92.6 %shard_map.128 = (bf16[512,512]{1,0:T(8,128)(2,1)}, bf16[512,512]{1,0:T(8,128)(2,1)}, bf16[512,512]{1,0:T(8,128)(2,1)}, f32[64,512]{1,0:T(8,128)}, f32[8,32]{1,0:T(8,128)}) custom-call(bf16[512,512]{1,0:T(8,128)(2,1)} %q_hbm.1, bf16[512,512]{1,0:T(8,128)(2,1)} %k_hbm.1, bf16[512,512]{1,0:T(8,128)(2,1)} %v_hbm.1, bf16[512,512]{1,0:T(8,128)(2,1)} %att_hbm.1, ...), custom_call_target="tpu_custom_call" | custom-call | tf_op jit(solution)/shard_map/pallas_call | solution.py:526
  94.6 0.0 copy-start.1
  94.6 1.9 %copy.19 = bf16[512,512]{1,0:T(8,128)(2,1)} copy(bf16[512,512]{1,0:T(8,128)(2,1)} %get-tuple-element.20) | data formatting | bytes 1048576
  96.6 0.0 copy-done.1
  96.6 0.0 copy-start
  96.6 0.8 copy.20
  97.4 0.4 copy-done
  97.8 0.0 copy-start.2
  97.8 0.8 copy.21
  98.6 0.2 copy-done.2
  98.8 0.0 copy-start.3
  98.8 0.7 copy.22
  99.5 0.0 copy-done.3
  99.5 0.6 copy.23
Async XLA Ops:
  0.6 0.7 copy-start.4
  94.6 1.9 %copy-start.1 = (bf16[512,512]{1,0:T(8,128)(2,1)S(1)}, bf16[512,512]{1,0:T(8,128)(2,1)}, u32[]{:S(2)}) copy-start(bf16[512,512]{1,0:T(8,128)(2,1)} %get-tuple-element.21) | copy-start | bytes 1572868
  96.6 1.2 %copy-start = (bf16[512,512]{1,0:T(8,128)(2,1)S(1)}, bf16[512,512]{1,0:T(8,128)(2,1)}, u32[]{:S(2)}) copy-start(bf16[512,512]{1,0:T(8,128)(2,1)} %get-tuple-element.22) | copy-start | bytes 1572868
  97.8 1.0 %copy-start.2 = (f32[64,512]{1,0:T(8,128)S(1)}, f32[64,512]{1,0:T(8,128)}, u32[]{:S(2)}) copy-start(f32[64,512]{1,0:T(8,128)} %get-tuple-element.23) | copy-start | bytes 393220
  98.8 0.7 copy-start.3

commit v2 on v1

--- a/solution.py
+++ b/solution.py
@@ -18,7 +18,9 @@
 WIDE = 768
 BLOCK = 128
 FAR = -4096.0
-N_SEM = 96
+N_SEM = 176
+UP_CUTS = 4
+UP_ROWS = 16
 
 
 def nt(a, b):
@@ -57,7 +59,9 @@
     q_hbm, k_hbm, v_hbm, att_hbm, up_hbm, wt_hbm, table_ref, bucket_ref, seg_ref,
     dq_ref, dk_ref, dv_ref, wg_ref, tg_ref,
     q_ref, k_ref, v_ref, att_ref, g_ref, ctx_ref, wa_ref, wb_ref, fp_ref, fm_ref,
-    ta_ref, tb_ref, rap_ref, ram_ref, sa_ref, saf_ref, rax_ref, ray_ref, say_ref,
+    ta_ref, tc_ref, tb_ref,
+    rap_ref, ram_ref, sa_ref, saf_ref, rax_ref, ray_ref, say_ref,
+    rcy_ref, rcp_ref, rcm_ref, sc_ref, scf_ref, rcx_ref,
     rbp_ref, rbm_ref, sby_ref, sbf_ref, rby_ref, sbz_ref, rbz_ref,
     e_ref, r_ref, dp_ref, pb_ref, dsb_ref, toe_ref, bext_ref, oh_ref, gb_ref, g8_ref,
     qaug_ref, kaug_ref, dqt_ref, dkp_ref, dvp_ref,
@@ -114,16 +118,15 @@
     pl.semaphore_wait(barrier, len(greeted))
 
     wire = Wire(send_sem, recv_sem)
-
-    y_pair = wire.send(wt_hbm.at[:, pl.ds(0, HALF)], wa_ref.at[z, yl, x], pair)
-    b_z = [
-        wire.send(wt_hbm.at[:, pl.ds(HALF, HALF)], wb_ref.at[z, yl, x], at_z(k)) for k in range(1, 8)
-    ]
+    got = {}
+
+    y_a = wire.send(wt_hbm.at[:, pl.ds(0, HALF)], wa_ref.at[z, yl, x], pair)
+    y_b = wire.send(wt_hbm.at[:, pl.ds(HALF, HALF)], wb_ref.at[z, yl, x], pair)
+    up_fp, up_fm = [], []
+    for c in range(UP_CUTS):
+        up_fp.append(wire.send(up_hbm.at[pl.ds(c * UP_ROWS, UP_ROWS), :], fp_ref.at[c], at_y(1)))
+        up_fm.append(wire.send(up_hbm.at[pl.ds(64 + c * UP_ROWS, UP_ROWS), :], fm_ref.at[c], at_y(3)))
     own_rows = pl.multiple_of(tensor * 128, 128)
-    up_fp, up_fm = [], []
-    for c in range(2):
-        up_fp.append(wire.send(up_hbm.at[pl.ds(c * 32, 32), :], fp_ref.at[c], at_y(1)))
-        up_fm.append(wire.send(up_hbm.at[pl.ds(64 + c * 32, 32), :], fm_ref.at[c], at_y(3)))
     to_mate = [wire.send(up_hbm, g_ref.at[pl.ds(own_rows, 128), :], mate)]
     for copy in loads:
         copy.wait()
@@ -131,17 +134,26 @@
     before = lax.div(lax.rem(y + 3, 4), 2) * 2 + core
     after = lax.div(lax.rem(y + 1, 4), 2) * 2 + core
     across = (1 - yh) * 2 + core
-    got = {}
-
-    def gather_a2():
-        y_pair.wait_recv()
+
+    def gather_first():
+        y_a.wait_recv()
+        y_b.wait_recv()
         got["a_x"] = [wire.send(wa_ref.at[z, :, x], wa_ref.at[z, :, x], at_x(k)) for k in (1, 3, 2)]
+        for way in (1, -1):
+            got["b_z", 1, way] = b_hop(1, way)
+        b_spread(0)
+
+    def far(step, way):
+        return zs(8 - step if way == 1 else step)
+
+    def z_next(way):
+        return at_z(1 if way == 1 else 7)
 
     def a_hop(step, way, part):
-        chunk = wa_ref.at[zs(8 - (step - 1) if way == 1 else step - 1), part]
-        return wire.send(chunk, chunk, at_z(1 if way == 1 else 7))
-
-    def gather_a3():
+        chunk = wa_ref.at[far(step - 1, way), part]
+        return wire.send(chunk, chunk, z_next(way))
+
+    def gather_a_start():
         for copy in got["a_x"]:
             copy.wait_recv()
         for part in range(2):
@@ -159,42 +171,58 @@
         got["a_z", 4, 1, 0].wait_recv()
         got["a_z", 4, -1, 1].wait_recv()
 
-    def gather_b2():
-        for copy in b_z:
-            copy.wait_recv()
-        got["b_y"] = wire.send(wb_ref.at[:, yl, x], wb_ref.at[:, yl, x], pair)
-
-    def gather_b3():
-        got["b_y"].wait_recv()
-        for part in range(2):
-            chunk = wb_ref.at[pl.ds(part * 4, 4), :, x]
-            for way in (1, 3):
-                got["b_x", 1, way, part] = wire.send(chunk, chunk, at_x(way))
-
-    def gather_b4(part):
-        for way in (1, 3):
-            got["b_x", 1, way, part].wait_recv()
-        way = 1 if part == 0 else 3
-        chunk = wb_ref.at[pl.ds(part * 4, 4), :, xs(3 if part == 0 else 1)]
-        got["b_x", 2, part] = wire.send(chunk, chunk, at_x(way))
+    def b_hop(step, way):
+        chunk = wb_ref.at[far(step - 1, way), :, x]
+        return wire.send(chunk, chunk, z_next(way))
+
+    def b_half_hop(way):
+        chunk = wb_ref.at[far(3, way), 0 if way == 1 else 1, x]
+        return wire.send(chunk, chunk, z_next(way))
+
+    def b_spread(k):
+        chunk = wb_ref.at[zs(k), :, x]
+        for side in (1, 3):
+            got["b_x", k, side] = wire.send(chunk, chunk, at_x(side))
+
+    def gather_b_step(step):
+        for way in (1, -1):
+            if step < 4:
+                got["b_z", step, way].wait_recv()
+            else:
+                got["b_z", 4, way].wait_recv()
+            if step < 3:
+                got["b_z", step + 1, way] = b_hop(step + 1, way)
+            elif step == 3:
+                got["b_z", 4, way] = b_half_hop(way)
+            if step < 4:
+                b_spread(8 - step if way == 1 else step)
+        if step == 4:
+            b_spread(4)
+
+    def gather_b_across(k):
+        for side in (1, 3):
+            got["b_x", k, side].wait_recv()
+            chunk = wb_ref.at[zs(k), 0 if side == 1 else 1, xs(3 if side == 1 else 1)]
+            got["b_x2", k, side] = wire.send(chunk, chunk, at_x(side))
 
     def gather_b_end():
-        for part in range(2):
-            got["b_x", 2, part].wait_recv()
-
-    def rows_of(owner, first, count):
-        return g_ref.at[pl.ds(pl.multiple_of(owner * 128 + first, 32), count), :]
+        for k in range(8):
+            for side in (1, 3):
+                got["b_x2", k, side].wait_recv()
+
+    def rows_of(owner, first):
+        return g_ref.at[pl.ds(pl.multiple_of(owner * 128 + first, UP_ROWS), UP_ROWS), :]
 
     def up_hand_on(c):
         up_fp[c].wait_recv()
-        got["u", 0, c] = wire.send(fp_ref.at[c], rows_of(before, c * 32, 32), at_y(1))
+        got["u", 0, c] = wire.send(fp_ref.at[c], rows_of(before, c * UP_ROWS), at_y(1))
         up_fm[c].wait_recv()
-        got["u", 1, c] = wire.send(fm_ref.at[c], rows_of(after, 64 + c * 32, 32), at_y(3))
+        got["u", 1, c] = wire.send(fm_ref.at[c], rows_of(after, 64 + c * UP_ROWS), at_y(3))
 
     def up_share(c):
         for side in range(2):
             got["u", side, c].wait_recv()
-            block = rows_of(across, side * 64 + c * 32, 32)
+            block = rows_of(across, side * 64 + c * UP_ROWS)
             to_mate.append(wire.send(block, block, mate))
 
     def up_end():
@@ -218,16 +246,16 @@
         dsb_ref[...] = jnp.zeros_like(dsb_ref)
 
     def columns(p):
-        return pl.ds(pl.multiple_of(p * BLOCK, BLOCK), BLOCK)
+        return pl.ds(p * BLOCK, BLOCK)
 
     def own_lanes(odd):
         lane = lax.broadcasted_iota(jnp.int32, (ROWS, BLOCK), 1)
         return (lane >= 64) if odd else (lane < 64)
 
-    def softmax_pair(p):
+    def softmax_head(h):
+        p, odd = h // 2, h % 2
         qp, kp = q_ref[:, columns(p)], k_ref[:, columns(p)]
-        for odd in range(2):
-            h = 2 * p + odd
+        if True:
             own = own_lanes(odd)
             q_h = jnp.where(own, qp, qaug_ref[...])
             k_h = jnp.where(own, kp, kaug_ref[...])
@@ -266,12 +294,12 @@
         rows = slice(m * 256, (m + 1) * 256)
         ctx_ref[rows, which * HALF : (which + 1) * HALF] = nn(g_ref[rows, :], w).astype(BF16)
 
-    def backward_pair(p):
+    def backward_head(h):
+        p, odd = h // 2, h % 2
         qp, kp = q_ref[:, columns(p)], k_ref[:, columns(p)]
         vp, gp = v_ref[:, columns(p)], ctx_ref[:, columns(p)]
         kpt = kp.T
-        for odd in range(2):
-            h = 2 * p + odd
+        if True:
             own = own_lanes(odd)
             g_h = jnp.where(own, gp, jnp.zeros_like(gp))
             delta = []
@@ -322,7 +350,8 @@
             else:
                 dk_ref[:, columns(p)] = jnp.where(own, dk_h, dkp_ref[...]).astype(BF16)
                 dv_ref[:, columns(p)] = jnp.where(own, dv_h, dvp_ref[...]).astype(BF16)
-        dq_ref[:, columns(p)] = dqt_ref[...].T.astype(BF16)
+        if odd == 1:
+            dq_ref[:, columns(p)] = dqt_ref[...].T.astype(BF16)
 
     def term(k):
         z_at = zs(k)
@@ -332,99 +361,122 @@
             (((0,), (0,)), ((), ())),
             preferred_element_type=F32,
         ).astype(BF16)
-        ta_ref[z_at] = block[:, :HALF].reshape(2, 4, 64, HALF)
+        ta_ref[z_at] = block[:, :BLOCK].reshape(2, 4, 64, BLOCK)
+        tc_ref[z_at] = block[:, BLOCK:HALF].reshape(2, 4, 64, BLOCK)
         tb_ref[z_at] = block[:, HALF:].reshape(2, 4, 64, HALF)
+
+    def total(*parts):
+        out = parts[0].astype(F32)
+        for part in parts[1:]:
+            out = out + part.astype(F32)
+        return out
 
     def sum_a_hop(k, way, part):
         come = rap_ref if way == 1 else ram_ref
         z_at = zs(k if way == 1 else 8 - k)
         if ("sa", k, way, part) in got:
             got["sa", k, way, part].wait_recv()
-            ta_ref[z_at, part] = (
-                ta_ref[z_at, part].astype(F32) + come[k, part].astype(F32)
-            ).astype(BF16)
+            ta_ref[z_at, part] = total(ta_ref[z_at, part], come[k, part]).astype(BF16)
         got["sa", k - 1, way, part] = wire.send(
-            ta_ref.at[z_at, part], come.at[k - 1, part], at_z(1 if way == 1 else 7)
+            ta_ref.at[z_at, part], come.at[k - 1, part], z_next(way)
         )
 
     def sum_a_step(k):
         for part in range(2):
             for way in (1, -1):
-                if k < 4 or (part == 0) == (way == 1):
-                    sum_a_hop(k, way, part)
-
-    def sum_a_x():
+                sum_a_hop(k, way, part)
+
+    def sum_a_x(part):
+        for way in (1, -1):
+            got["sa", 0, way, part].wait_recv()
+        full = total(ta_ref[z, part], rap_ref[0, part], ram_ref[0, part])
+        saf_ref[part] = full
+        sa_ref[part] = full.astype(BF16)
+        for k in (2, 1, 3):
+            got["sax", part, k] = wire.send(sa_ref.at[part, xs(k)], rax_ref.at[part, k - 1], at_x(k))
+
+    def sum_a_y():
         for part in range(2):
-            for way in (1, -1):
-                got["sa", 0, way, part].wait_recv()
-            full = (
-                ta_ref[z, part].astype(F32) + rap_ref[0, part].astype(F32) + ram_ref[0, part].astype(F32)
-            )
-            saf_ref[part] = full
-            sa_ref[part] = full.astype(BF16)
-        for k in (1, 3, 2):
-            got["sax", k] = wire.send(sa_ref.at[:, xs(k)], rax_ref.at[k - 1], at_x(k))
-
-    def sum_a_y():
-        full = saf_ref[:, x]
-        for k in (1, 3, 2):
-            got["sax", k].wait_recv()
-            full = full + rax_ref[k - 1].astype(F32)
-        saf_ref[:, x] = full
-        say_ref[...] = full.astype(BF16)
+            full = saf_ref[part, x]
+            for k in (1, 3, 2):
+                got["sax", part, k].wait_recv()
+                full = full + rax_ref[part, k - 1].astype(F32)
+            saf_ref[part, x] = full
+            say_ref[part] = full.astype(BF16)
         got["say"] = wire.send(say_ref.at[1 - yl], ray_ref, pair)
 
     def sum_a_end():
         got["say"].wait_recv()
-        wg_ref[:, :HALF] = saf_ref[yl, x] + ray_ref[...].astype(F32)
-
-    def part_b(part):
-        return pl.ds(part * 4, 4)
-
-    def sum_b_first():
-        got["sb", 1, 1, 0] = wire.send(tb_ref.at[part_b(0), :, xs(2)], rbp_ref.at[1], at_x(1))
-        got["sb", 1, 3, 1] = wire.send(tb_ref.at[part_b(1), :, xs(2)], rbm_ref.at[1], at_x(3))
-        sum_b_hop(1, 1)
-        sum_b_hop(3, 0)
-
-    def sum_b_hop(way, part):
-        come = rbp_ref if way == 1 else rbm_ref
-        if ("sb", 1, way, part) in got:
-            got["sb", 1, way, part].wait_recv()
-            at = (part_b(part), slice(None), xs(way))
-            tb_ref[at] = (tb_ref[at].astype(F32) + come[1].astype(F32)).astype(BF16)
-        got["sb", 0, way, part] = wire.send(
-            tb_ref.at[part_b(part), :, xs(way)],
-            (come.at[0] if (part == 0) == (way == 1) else come.at[2]),
-            at_x(way),
-        )
-
-    def sum_b_second():
-        sum_b_hop(1, 0)
-        sum_b_hop(3, 1)
-
-    def sum_b_y():
-        for part in (1, 0):
-            for way in (1, 3):
-                got["sb", 0, way, part].wait_recv()
-        for part in range(2):
-            up = rbp_ref[0 if part == 0 else 2].astype(F32)
-            down = rbm_ref[2 if part == 0 else 0].astype(F32)
-            full = tb_ref[part_b(part), :, x].astype(F32) + up + down
-            sbf_ref[part_b(part)] = full
-            sby_ref[part_b(part)] = full.astype(BF16)
-        got["sby"] = wire.send(sby_ref.at[:, 1 - yl], rby_ref, pair)
-
-    def sum_b_z():
-        got["sby"].wait_recv()
-        full = sbf_ref[:, yl] + rby_ref[...].astype(F32)
-        sbf_ref[:, 0] = full
-        sbz_ref[...] = full.astype(BF16)
-        for k in range(1, 8):
-            got["sbz", k] = wire.send(sbz_ref.at[zs(k)], rbz_ref.at[k - 1], at_z(k))
+        wg_ref[:, :BLOCK] = total(saf_ref[yl, x], ray_ref[...])
+
+    def sum_c_y(k):
+        got["scy", k] = wire.send(tc_ref.at[zs(k), 1 - yl], rcy_ref.at[k], pair)
+
+    def sum_c_hop(k, way):
+        come = rcp_ref if way == 1 else rcm_ref
+        rel = k if way == 1 else 8 - k
+        got["scy", rel].wait_recv()
+        parts = [tc_ref[zs(rel), yl], rcy_ref[rel]]
+        if ("sc", k, way) in got:
+            got["sc", k, way].wait_recv()
+            parts.append(come[k])
+        tc_ref[zs(rel), yl] = total(*parts).astype(BF16)
+        got["sc", k - 1, way] = wire.send(tc_ref.at[zs(rel), yl], come.at[k - 1], z_next(way))
+
+    def sum_c_step(k):
+        for way in (1, -1):
+            sum_c_hop(k, way)
+
+    def sum_c_x():
+        got["scy", 0].wait_recv()
+        for way in (1, -1):
+            got["sc", 0, way].wait_recv()
+        full = total(tc_ref[z, yl], rcy_ref[0], rcp_ref[0], rcm_ref[0])
+        scf_ref[...] = full
+        sc_ref[...] = full.astype(BF16)
+        for k in (2, 1, 3):
+            got["scx", k] = wire.send(sc_ref.at[xs(k)], rcx_ref.at[k - 1], at_x(k))
+
+    def sum_c_end():
+        full = scf_ref[x]
+        for k in (1, 3, 2):
+            got["scx", k].wait_recv()
+            full = full + rcx_ref[k - 1].astype(F32)
+        wg_ref[:, BLOCK:HALF] = full
+
+    def sum_b_first(k, side):
+        other = 4 - side
+        come = rbp_ref if side == 1 else rbm_ref
+        back = rbm_ref if side == 1 else rbp_ref
+        got["sb2", k] = wire.send(tb_ref.at[zs(k), :, xs(2)], come.at[k, 1], at_x(side))
+        got["sb1", k, other] = wire.send(tb_ref.at[zs(k), :, xs(other)], back.at[k, 0], at_x(other))
+
+    def sum_b_second(k, side):
+        come = rbp_ref if side == 1 else rbm_ref
+        got["sb2", k].wait_recv()
+        at = (zs(k), slice(None), xs(side))
+        tb_ref[at] = total(tb_ref[at], come[k, 1]).astype(BF16)
+        got["sb1", k, side] = wire.send(tb_ref.at[at], come.at[k, 0], at_x(side))
+
+    def sum_b_y(k):
+        for side in (1, 3):
+            got["sb1", k, side].wait_recv()
+        full = total(tb_ref[zs(k), :, x], rbp_ref[k, 0], rbm_ref[k, 0])
+        sbf_ref[k] = full
+        sby_ref[k] = full.astype(BF16)
+        got["sby", k] = wire.send(sby_ref.at[k, 1 - yl], rby_ref.at[k], pair)
+
+    def sum_b_z(k):
+        got["sby", k].wait_recv()
+        full = total(sbf_ref[k, yl], rby_ref[k])
+        if k:
+            sbz_ref[k] = full.astype(BF16)
+            got["sbz", k] = wire.send(sbz_ref.at[k], rbz_ref.at[k - 1], at_z(k))
+        else:
+            sbf_ref[0, 0] = full
 
     def sum_b_end():
-        full = sbf_ref[z, 0]
+        full = sbf_ref[0, 0]
         for k in range(1, 8):
             got["sbz", k].wait_recv()
             full = full + rbz_ref[k - 1].astype(F32)
@@ -461,55 +513,112 @@
         tg_ref[...] = (ty_ref[...] + rty_ref[...])[:, :32]
 
     prepare()
-    gather_a2()
-    gather_a3()
-    gather_b2()
-    softmax_pair(0)
+    gather_first()
+    softmax_head(0)
     up_hand_on(0)
+    gather_a_start()
+    gather_b_step(1)
+    gather_b_across(0)
+    softmax_head(1)
+    up_hand_on(1)
+    softmax_head(2)
+    up_hand_on(2)
+    gather_b_step(2)
+    softmax_head(3)
+    gather_b_across(1)
+    gather_b_across(7)
+    up_hand_on(3)
     gather_a_step(1)
-    gather_b3()
-    up_hand_on(1)
-    softmax_pair(1)
+    softmax_head(4)
+    gather_b_step(3)
+    up_share(0)
+    softmax_head(5)
+    gather_b_across(2)
+    gather_b_across(6)
+    up_share(1)
+    gather_b_step(4)
     gather_a_step(2)
-    up_share(0)
-    softmax_pair(2)
-    gather_b4(0)
+    softmax_head(6)
+    up_share(2)
+    gather_b_across(3)
+    gather_b_across(5)
+    softmax_head(7)
+    up_share(3)
+    up_end()
+    term(4)
+    sum_a_hop(4, 1, 0)
+    sum_a_hop(4, -1, 1)
+    sum_c_y(4)
+    sum_b_first(4, 1)
     gather_a_step(3)
-    gather_b4(1)
-    up_share(1)
-    softmax_pair(3)
-    up_end()
-    for k in (4, 3, 5):
+    gather_b_across(4)
+    term(3)
+    sum_a_hop(3, 1, 1)
+    sum_c_y(3)
+    sum_b_first(3, 3)
+    term(5)
+    sum_a_hop(3, -1, 0)
+    sum_c_y(5)
+    sum_b_first(5, 1)
+    term(2)
+    sum_c_y(2)
+    sum_b_first(2, 3)
+    sum_a_hop(3, 1, 0)
+    sum_a_hop(3, -1, 1)
+    sum_c_hop(4, 1)
+    for k, side in ((6, 1), (1, 3), (7, 1), (0, 3)):
         term(k)
-        if k == 4:
-            sum_a_step(4)
-    for part in range(2):
-        for way in (1, -1):
-            if ("sa", 3, way, part) not in got:
-                sum_a_hop(3, way, part)
-    for k in (2, 6, 1, 7, 0):
-        term(k)
-    sum_b_first()
-    for part, way in ((0, 1), (1, -1)):
-        sum_a_hop(3, way, part)
+        sum_c_y(k)
+        sum_b_first(k, side)
     gather_a_end()
     context(0, 0)
     context(0, 1)
+    sum_a_step(2)
+    sum_c_step(3)
+    sum_b_second(4, 1)
+    sum_b_second(3, 3)
     gather_b_end()
-    sum_a_step(2)
     context(1, 0)
     context(1, 1)
-    sum_b_second()
-    backward_pair(0)
+    backward_head(0)
     sum_a_step(1)
-    backward_pair(1)
-    sum_b_y()
-    sum_a_x()
-    backward_pair(2)
-    sum_b_z()
+    sum_c_step(2)
+    sum_b_second(5, 1)
+    sum_b_second(2, 3)
+    backward_head(1)
+    backward_head(2)
+    sum_b_second(6, 1)
+    sum_b_second(1, 3)
+    sum_c_step(1)
+    sum_a_x(0)
+    sum_a_x(1)
+    backward_head(3)
+    sum_b_second(7, 1)
+    sum_b_second(0, 3)
+    sum_b_y(4)
+    sum_b_y(3)
+    backward_head(4)
+    sum_c_x()
     sum_a_y()
-    backward_pair(3)
+    sum_b_y(5)
+    sum_b_y(2)
+    sum_b_z(4)
+    sum_b_z(3)
+    backward_head(5)
+    sum_b_y(6)
+    sum_b_y(1)
+    sum_b_z(5)
+    sum_b_z(2)
+    sum_b_y(7)
+    sum_b_y(0)
+    backward_head(6)
+    sum_b_z(6)
+    sum_b_z(1)
+    backward_head(7)
     table_z()
+    sum_b_z(7)
+    sum_b_z(0)
+    sum_c_end()
     sum_a_end()
     table_x()
     sum_b_end()
@@ -518,32 +627,45 @@
     wire.finish()
 
 
+def carry(*refs):
+    sems = refs[-1]
+    pairs = zip(refs[:5], refs[5:10])
+    copies = [pltpu.make_async_copy(src, dst, sems.at[at]) for at, (src, dst) in enumerate(pairs)]
+    for copy in copies:
+        copy.start()
+    for copy in copies:
+        copy.wait()
+
+
 def on_device(queries, keys, values, attended, upstream, out_weight, bias_table, buckets, segments):
     shifted = jnp.pad(buckets, (129, WIDE - 129 - buckets.shape[0]), constant_values=-1)[None, :]
     anywhere = pl.BlockSpec(memory_space=pl.ANY)
     inside = pl.BlockSpec(memory_space=pltpu.VMEM)
     bf, f4 = (lambda *s: pltpu.VMEM(s, BF16)), (lambda *s: pltpu.VMEM(s, F32))
-    dq, dk, dv, wg, tg = pl.pallas_call(
+    shapes = (
+        jax.ShapeDtypeStruct((ROWS, FEAT), BF16),
+        jax.ShapeDtypeStruct((ROWS, FEAT), BF16),
+        jax.ShapeDtypeStruct((ROWS, FEAT), BF16),
+        jax.ShapeDtypeStruct((64, FEAT), F32),
+        jax.ShapeDtypeStruct((HEADS, 32), F32),
+    )
+    made = pl.pallas_call(
         kernel,
-        out_shape=(
-            jax.ShapeDtypeStruct((ROWS, FEAT), BF16),
-            jax.ShapeDtypeStruct((ROWS, FEAT), BF16),
-            jax.ShapeDtypeStruct((ROWS, FEAT), BF16),
-            jax.ShapeDtypeStruct((64, FEAT), F32),
-            jax.ShapeDtypeStruct((HEADS, 32), F32),
-        ),
+        out_shape=shapes,
         in_specs=[anywhere] * 6 + [inside] * 3,
         out_specs=(inside,) * 5,
         scratch_shapes=[
             bf(ROWS, FEAT), bf(ROWS, FEAT), bf(ROWS, FEAT), bf(ROWS, FEAT),
             bf(ROWS, D), bf(ROWS, FEAT),
             bf(8, 2, 4, 64, HALF), bf(8, 2, 4, 64, HALF),
-            bf(2, 32, D), bf(2, 32, D),
-            bf(8, 2, 4, 64, HALF), bf(8, 2, 4, 64, HALF),
-            bf(4, 2, 4, 64, HALF), bf(4, 2, 4, 64, HALF),
-            bf(2, 4, 64, HALF), f4(2, 4, 64, HALF), bf(3, 2, 64, HALF), bf(64, HALF), bf(2, 64, HALF),
-            bf(3, 4, 2, 64, HALF), bf(3, 4, 2, 64, HALF),
-            bf(8, 2, 64, HALF), f4(8, 2, 64, HALF), bf(8, 64, HALF), bf(8, 64, HALF), bf(7, 64, HALF),
+            bf(UP_CUTS, UP_ROWS, D), bf(UP_CUTS, UP_ROWS, D),
+            bf(8, 2, 4, 64, BLOCK), bf(8, 2, 4, 64, BLOCK), bf(8, 2, 4, 64, HALF),
+            bf(4, 2, 4, 64, BLOCK), bf(4, 2, 4, 64, BLOCK), bf(2, 4, 64, BLOCK), f4(2, 4, 64, BLOCK),
+            bf(2, 3, 64, BLOCK), bf(64, BLOCK), bf(2, 64, BLOCK),
+            bf(8, 4, 64, BLOCK), bf(4, 4, 64, BLOCK), bf(4, 4, 64, BLOCK), bf(4, 64, BLOCK),
+            f4(4, 64, BLOCK), bf(3, 64, BLOCK),
+            bf(8, 2, 2, 64, HALF), bf(8, 2, 2, 64, HALF), bf(8, 2, 64, HALF), f4(8, 2, 64, HALF),
+            bf(8, 64, HALF), bf(8, 64, HALF), bf(7, 64, HALF),
             f4(HEADS, ROWS, ROWS), f4(HEADS, ROWS), f4(ROWS, ROWS), bf(ROWS, ROWS), bf(ROWS, ROWS),
             f4(5, BLOCK, BLOCK), f4(HEADS, WIDE), f4(32, WIDE), f4(HEADS, WIDE), f4(8, WIDE),
             bf(ROWS, BLOCK), bf(ROWS, BLOCK), f4(BLOCK, ROWS), f4(ROWS, BLOCK), f4(ROWS, BLOCK),
@@ -559,6 +681,13 @@
     )(
         queries, keys, values, attended, upstream, out_weight.T, bias_table.T, shifted, segments[None, :]
     )
+    dq, dk, dv, wg, tg = pl.pallas_call(
+        carry,
+        out_shape=shapes,
+        in_specs=[anywhere] * 5,
+        out_specs=(anywhere,) * 5,
+        scratch_shapes=[pltpu.SemaphoreType.DMA((5,))],
+    )(*made)
     return dq, dk, dv, wg, tg.T
 
 

time: 100 us -> 142 us (1.42)
  Pallas kernels: 92.6 us -> 140 us
  local copies, waits for them, and re-layouts: 6.79 us -> 1.33 us
    pallas_call x1 -> x2, Pallas kernels: 92.6 us -> 140 us  [the longest x1 86.8 us: on_device(): pl.pallas_call(kernel, out_shape=shapes, in_specs=[anywhere] * 6 + [insid...]
    unnamed x15 -> x2, local copies, waits for them, and re-layouts: 6.13 us -> 0.67 us
where the time goes in v2:
time: 142 us
  Pallas kernels  140 us (99%)
    pallas_call x1, Pallas kernels, on_device(): pl.pallas_call(kernel, out_shape=shapes, in_specs=[anywhere] * 6 + [insid...  86.8 us
    pallas_call x1, Pallas kernels, on_device(): pl.pallas_call(carry, out_shape=shapes, in_specs=[anywhere] * 5, out_spec...  52.9 us

profile of v2, /device:TPU:16, one launch (start us, length us, event | category | flops | bytes accessed | tf_op | source)
XLA Modules:
  0.0 141.8 jit_solution(17405199798342883218)
XLA Ops:
  0.6 0.0 copy-start
  0.6 0.7 copy-done
  1.3 0.1 pad.4
  1.4 0.6 broadcast_in_dim.6.bucket_ref
  2.0 86.8 %shard_map.128 = (bf16[512,512]{1,0:T(8,128)(2,1)}, bf16[512,512]{1,0:T(8,128)(2,1)}, bf16[512,512]{1,0:T(8,128)(2,1)}, f32[64,512]{1,0:T(8,128)}, f32[8,32]{1,0:T(8,128)}) custom-call(bf16[512,512]{1,0:T(8,128)(2,1)} %q_hbm.1, bf16[512,512]{1,0:T(8,128)(2,1)} %k_hbm.1, bf16[512,512]{1,0:T(8,128)(2,1)} %v_hbm.1, bf16[512,512]{1,0:T(8,128)(2,1)} %att_hbm.1, ...), custom_call_target="tpu_custom_call" | custom-call | tf_op jit(solution)/shard_map/pallas_call | solution.py:652
  88.7 52.9 %shard_map.129 = (bf16[512,512]{1,0:T(8,128)(2,1)}, bf16[512,512]{1,0:T(8,128)(2,1)}, bf16[512,512]{1,0:T(8,128)(2,1)}, f32[64,512]{1,0:T(8,128)}, f32[8,32]{1,0:T(8,128)}) custom-call(bf16[512,512]{1,0:T(8,128)(2,1)} %get-tuple-element.15.refs_0_, bf16[512,512]{1,0:T(8,128)(2,1)} %get-tuple-element.16.refs_1_, bf16[512,512]{1,0:T(8,128)(2,1)} %get-tuple-element.17.refs_2_, ...), custom_call_target="tpu_custom_call" | custom-call | tf_op jit(solution)/shard_map/pallas_call | solution.py:684
Async XLA Ops:
  0.6 0.7 copy-start

commit v3 on v2

--- a/solution.py
+++ b/solution.py
@@ -1,5 +1,3 @@
-import functools
-
 import jax
 import jax.numpy as jnp
 from jax import lax
@@ -18,9 +16,9 @@
 WIDE = 768
 BLOCK = 128
 FAR = -4096.0
-N_SEM = 176
-UP_CUTS = 4
-UP_ROWS = 16
+N_SEM = 224
+KS = (4, 3, 5, 2, 6, 1, 7, 0)
+WINDOW = 3
 
 
 def nt(a, b):
@@ -65,7 +63,7 @@
     rbp_ref, rbm_ref, sby_ref, sbf_ref, rby_ref, sbz_ref, rbz_ref,
     e_ref, r_ref, dp_ref, pb_ref, dsb_ref, toe_ref, bext_ref, oh_ref, gb_ref, g8_ref,
     qaug_ref, kaug_ref, dqt_ref, dkp_ref, dvp_ref,
-    tz_ref, rtz_ref, tx_ref, rtx_ref, ty_ref, rty_ref,
+    tz_ref, rtz_ref, tx_ref, rtx_ref,
     local_sem, send_sem, recv_sem,
 ):
     me, tensor = lax.axis_index("dp"), lax.axis_index("tensor")
@@ -112,7 +110,8 @@
         loads.append(copy)
 
     barrier = pltpu.get_barrier_semaphore()
-    greeted = [at_z(k) for k in range(1, 8)] + [at_x(k) for k in range(1, 4)] + [at_y(1), at_y(3), mate]
+    around = [at_x(k) for k in range(1, 4)] + [place(z, 1 - yl, xs(k), yh, core) for k in range(4)]
+    greeted = [at_z(k) for k in range(1, 8)] + around + [place(z, 1 - yl, x, 1 - yh, core), mate]
     for device in greeted:
         pl.semaphore_signal(barrier, inc=1, device_id=device, device_id_type=MESH)
     pl.semaphore_wait(barrier, len(greeted))
@@ -122,12 +121,19 @@
 
     y_a = wire.send(wt_hbm.at[:, pl.ds(0, HALF)], wa_ref.at[z, yl, x], pair)
     y_b = wire.send(wt_hbm.at[:, pl.ds(HALF, HALF)], wb_ref.at[z, yl, x], pair)
-    up_fp, up_fm = [], []
-    for c in range(UP_CUTS):
-        up_fp.append(wire.send(up_hbm.at[pl.ds(c * UP_ROWS, UP_ROWS), :], fp_ref.at[c], at_y(1)))
-        up_fm.append(wire.send(up_hbm.at[pl.ds(64 + c * UP_ROWS, UP_ROWS), :], fm_ref.at[c], at_y(3)))
+    up_fp, up_fm = {}, {}
+
+    def cols(k):
+        return pl.ds(pl.multiple_of(zs(k) * FEAT, FEAT), FEAT)
+
+    def up_first(i):
+        up_fp[i] = wire.send(up_hbm.at[pl.ds(0, 64), cols(KS[i])], fp_ref.at[i], at_y(1))
+        up_fm[i] = wire.send(up_hbm.at[pl.ds(64, 64), cols(KS[i])], fm_ref.at[i], at_y(3))
+
+    for i in range(WINDOW):
+        up_first(i)
     own_rows = pl.multiple_of(tensor * 128, 128)
-    to_mate = [wire.send(up_hbm, g_ref.at[pl.ds(own_rows, 128), :], mate)]
+    to_mate = wire.send(up_hbm, g_ref.at[pl.ds(own_rows, 128), :], mate)
     for copy in loads:
         copy.wait()
 
@@ -141,6 +147,7 @@
         got["a_x"] = [wire.send(wa_ref.at[z, :, x], wa_ref.at[z, :, x], at_x(k)) for k in (1, 3, 2)]
         for way in (1, -1):
             got["b_z", 1, way] = b_hop(1, way)
+            got["a_z", 1, way, 0] = a_hop(1, way, 0)
         b_spread(0)
 
     def far(step, way):
@@ -150,26 +157,25 @@
         return at_z(1 if way == 1 else 7)
 
     def a_hop(step, way, part):
-        chunk = wa_ref.at[far(step - 1, way), part]
+        chunk = wa_ref.at[far(step - 1, way), :, xs(part)]
         return wire.send(chunk, chunk, z_next(way))
 
     def gather_a_start():
-        for copy in got["a_x"]:
+        for copy, part in zip(got["a_x"], (3, 1, 2)):
             copy.wait_recv()
-        for part in range(2):
             for way in (1, -1):
                 got["a_z", 1, way, part] = a_hop(1, way, part)
 
     def gather_a_step(step):
-        for part in range(2):
+        for part in (0, 3, 1, 2):
             for way in (1, -1):
                 got["a_z", step, way, part].wait_recv()
-                if step < 3 or (part == 0) == (way == 1):
+                if step < 3 or (part in (0, 3)) == (way == 1):
                     got["a_z", step + 1, way, part] = a_hop(step + 1, way, part)
 
     def gather_a_end():
-        got["a_z", 4, 1, 0].wait_recv()
-        got["a_z", 4, -1, 1].wait_recv()
+        for part, way in ((0, 1), (3, 1), (1, -1), (2, -1)):
+            got["a_z", 4, way, part].wait_recv()
 
     def b_hop(step, way):
         chunk = wb_ref.at[far(step - 1, way), :, x]
@@ -210,24 +216,28 @@
             for side in (1, 3):
                 got["b_x2", k, side].wait_recv()
 
-    def rows_of(owner, first):
-        return g_ref.at[pl.ds(pl.multiple_of(owner * 128 + first, UP_ROWS), UP_ROWS), :]
-
-    def up_hand_on(c):
-        up_fp[c].wait_recv()
-        got["u", 0, c] = wire.send(fp_ref.at[c], rows_of(before, c * UP_ROWS), at_y(1))
-        up_fm[c].wait_recv()
-        got["u", 1, c] = wire.send(fm_ref.at[c], rows_of(after, 64 + c * UP_ROWS), at_y(3))
-
-    def up_share(c):
+    def block_of(owner, first, k):
+        return g_ref.at[pl.ds(pl.multiple_of(owner * 128 + first, 64), 64), cols(k)]
+
+    def up_hand_on(i):
+        up_fp[i].wait_recv()
+        got["u", 0, i] = wire.send(fp_ref.at[i], block_of(before, 0, KS[i]), at_y(1))
+        up_fm[i].wait_recv()
+        got["u", 1, i] = wire.send(fm_ref.at[i], block_of(after, 64, KS[i]), at_y(3))
+        if i + WINDOW < 8:
+            up_first(i + WINDOW)
+
+    def up_share(i):
         for side in range(2):
-            got["u", side, c].wait_recv()
-            block = rows_of(across, side * 64 + c * UP_ROWS)
-            to_mate.append(wire.send(block, block, mate))
-
-    def up_end():
-        for copy in to_mate:
-            copy.wait_recv()
+            got["u", side, i].wait_recv()
+            block = block_of(across, side * 64, KS[i])
+            got["us", side, i] = wire.send(block, block, mate)
+
+    def up_end(i):
+        if i == 0:
+            to_mate.wait_recv()
+        for side in range(2):
+            got["us", side, i].wait_recv()
 
     def prepare():
         lane = lax.broadcasted_iota(jnp.int32, (ROWS, BLOCK), 1)
@@ -491,150 +501,156 @@
         for k in range(1, 8):
             got["tz", k] = wire.send(tz_ref, rtz_ref.at[k - 1], at_z(k))
 
-    def table_x():
+    def table_xy():
         full = tz_ref[...]
         for k in range(1, 8):
             got["tz", k].wait_recv()
             full = full + rtz_ref[k - 1]
         tx_ref[...] = full
-        for k in range(1, 4):
-            got["tx", k] = wire.send(tx_ref, rtx_ref.at[k - 1], at_x(k))
-
-    def table_y():
+        for k, device in enumerate(around):
+            got["tx", k] = wire.send(tx_ref, rtx_ref.at[k], device)
+
+    def table_end():
         full = tx_ref[...]
-        for k in range(1, 4):
+        for k in range(7):
             got["tx", k].wait_recv()
-            full = full + rtx_ref[k - 1]
-        ty_ref[...] = full
-        got["ty"] = wire.send(ty_ref, rty_ref, pair)
-
-    def table_end():
-        got["ty"].wait_recv()
-        tg_ref[...] = (ty_ref[...] + rty_ref[...])[:, :32]
+            full = full + rtx_ref[k]
+        tg_ref[...] = full[:, :32]
+
+    def sums_start(i):
+        k = KS[i]
+        term(k)
+        if k == 4:
+            sum_a_hop(4, 1, 0)
+            sum_a_hop(4, -1, 1)
+        if k == 3:
+            sum_a_hop(3, 1, 1)
+        if k == 5:
+            sum_a_hop(3, -1, 0)
+        sum_c_y(k)
+        sum_b_first(k, 1 if i % 2 == 0 else 3)
 
     prepare()
     gather_first()
+    up_hand_on(0)
     softmax_head(0)
-    up_hand_on(0)
+    up_hand_on(1)
+    gather_b_step(1)
     gather_a_start()
-    gather_b_step(1)
+    up_hand_on(2)
+    softmax_head(1)
     gather_b_across(0)
-    softmax_head(1)
-    up_hand_on(1)
-    softmax_head(2)
-    up_hand_on(2)
+    up_share(0)
     gather_b_step(2)
-    softmax_head(3)
+
+    up_end(0)
+    sums_start(0)
+    up_hand_on(3)
+    up_share(1)
     gather_b_across(1)
     gather_b_across(7)
-    up_hand_on(3)
+    softmax_head(2)
+    up_end(1)
+    sums_start(1)
+    up_hand_on(4)
+    up_share(2)
     gather_a_step(1)
-    softmax_head(4)
+    softmax_head(3)
+    up_end(2)
+    sums_start(2)
+    up_hand_on(5)
+    up_share(3)
     gather_b_step(3)
-    up_share(0)
-    softmax_head(5)
     gather_b_across(2)
     gather_b_across(6)
-    up_share(1)
-    gather_b_step(4)
-    gather_a_step(2)
-    softmax_head(6)
-    up_share(2)
-    gather_b_across(3)
-    gather_b_across(5)
-    softmax_head(7)
-    up_share(3)
-    up_end()
-    term(4)
-    sum_a_hop(4, 1, 0)
-    sum_a_hop(4, -1, 1)
-    sum_c_y(4)
-    sum_b_first(4, 1)
-    gather_a_step(3)
-    gather_b_across(4)
-    term(3)
-    sum_a_hop(3, 1, 1)
-    sum_c_y(3)
-    sum_b_first(3, 3)
-    term(5)
-    sum_a_hop(3, -1, 0)
-    sum_c_y(5)
-    sum_b_first(5, 1)
-    term(2)
-    sum_c_y(2)
-    sum_b_first(2, 3)
+    softmax_head(4)
+    up_end(3)
+    sums_start(3)
+    up_hand_on(6)
+    up_share(4)
     sum_a_hop(3, 1, 0)
     sum_a_hop(3, -1, 1)
     sum_c_hop(4, 1)
-    for k, side in ((6, 1), (1, 3), (7, 1), (0, 3)):
-        term(k)
-        sum_c_y(k)
-        sum_b_first(k, side)
+    gather_a_step(2)
+    softmax_head(5)
+    up_end(4)
+    sums_start(4)
+    up_hand_on(7)
+    up_share(5)
+    gather_b_step(4)
+    gather_b_across(3)
+    gather_b_across(5)
+    sum_b_second(4, 1)
+    sum_b_second(3, 3)
+    softmax_head(6)
+    up_end(5)
+    sums_start(5)
+    up_share(6)
+    sum_a_step(2)
+    sum_c_step(3)
+    gather_a_step(3)
+    softmax_head(7)
+    up_end(6)
+    sums_start(6)
+    up_share(7)
+    gather_b_across(4)
+    sum_b_second(5, 1)
+    sum_b_second(2, 3)
+    sum_b_y(4)
+    sum_b_y(3)
+    up_end(7)
+    sums_start(7)
+    sum_a_step(1)
+    sum_c_step(2)
+    sum_b_second(6, 1)
+    sum_b_second(1, 3)
     gather_a_end()
     context(0, 0)
     context(0, 1)
-    sum_a_step(2)
-    sum_c_step(3)
-    sum_b_second(4, 1)
-    sum_b_second(3, 3)
     gather_b_end()
     context(1, 0)
     context(1, 1)
     backward_head(0)
-    sum_a_step(1)
-    sum_c_step(2)
-    sum_b_second(5, 1)
-    sum_b_second(2, 3)
-    backward_head(1)
-    backward_head(2)
-    sum_b_second(6, 1)
-    sum_b_second(1, 3)
-    sum_c_step(1)
-    sum_a_x(0)
-    sum_a_x(1)
-    backward_head(3)
     sum_b_second(7, 1)
     sum_b_second(0, 3)
-    sum_b_y(4)
-    sum_b_y(3)
-    backward_head(4)
-    sum_c_x()
-    sum_a_y()
+    backward_head(1)
+    sum_c_step(1)
+    backward_head(2)
     sum_b_y(5)
     sum_b_y(2)
     sum_b_z(4)
     sum_b_z(3)
-    backward_head(5)
+    backward_head(3)
+    sum_a_x(0)
+    sum_a_x(1)
+    backward_head(4)
     sum_b_y(6)
     sum_b_y(1)
     sum_b_z(5)
     sum_b_z(2)
+    backward_head(5)
+    sum_c_x()
+    sum_a_y()
+    backward_head(6)
     sum_b_y(7)
     sum_b_y(0)
-    backward_head(6)
+    backward_head(7)
+    table_z()
     sum_b_z(6)
     sum_b_z(1)
-    backward_head(7)
-    table_z()
     sum_b_z(7)
     sum_b_z(0)
     sum_c_end()
+    table_xy()
     sum_a_end()
-    table_x()
     sum_b_end()
-    table_y()
     table_end()
     wire.finish()
 
 
 def carry(*refs):
-    sems = refs[-1]
-    pairs = zip(refs[:5], refs[5:10])
-    copies = [pltpu.make_async_copy(src, dst, sems.at[at]) for at, (src, dst) in enumerate(pairs)]
-    for copy in copies:
-        copy.start()
-    for copy in copies:
-        copy.wait()
+    for src, dst in zip(refs[:5], refs[5:]):
+        dst[...] = src[...]
 
 
 def on_device(queries, keys, values, attended, upstream, out_weight, bias_table, buckets, segments):
@@ -658,7 +674,7 @@
             bf(ROWS, FEAT), bf(ROWS, FEAT), bf(ROWS, FEAT), bf(ROWS, FEAT),
             bf(ROWS, D), bf(ROWS, FEAT),
             bf(8, 2, 4, 64, HALF), bf(8, 2, 4, 64, HALF),
-            bf(UP_CUTS, UP_ROWS, D), bf(UP_CUTS, UP_ROWS, D),
+            bf(8, 64, FEAT), bf(8, 64, FEAT),
             bf(8, 2, 4, 64, BLOCK), bf(8, 2, 4, 64, BLOCK), bf(8, 2, 4, 64, HALF),
             bf(4, 2, 4, 64, BLOCK), bf(4, 2, 4, 64, BLOCK), bf(2, 4, 64, BLOCK), f4(2, 4, 64, BLOCK),
             bf(2, 3, 64, BLOCK), bf(64, BLOCK), bf(2, 64, BLOCK),
@@ -669,8 +685,7 @@
             f4(HEADS, ROWS, ROWS), f4(HEADS, ROWS), f4(ROWS, ROWS), bf(ROWS, ROWS), bf(ROWS, ROWS),
             f4(5, BLOCK, BLOCK), f4(HEADS, WIDE), f4(32, WIDE), f4(HEADS, WIDE), f4(8, WIDE),
             bf(ROWS, BLOCK), bf(ROWS, BLOCK), f4(BLOCK, ROWS), f4(ROWS, BLOCK), f4(ROWS, BLOCK),
-            f4(HEADS, BLOCK), f4(7, HEADS, BLOCK), f4(HEADS, BLOCK), f4(3, HEADS, BLOCK),
-            f4(HEADS, BLOCK), f4(HEADS, BLOCK),
+            f4(HEADS, BLOCK), f4(7, HEADS, BLOCK), f4(HEADS, BLOCK), f4(7, HEADS, BLOCK),
             pltpu.SemaphoreType.DMA((7,)),
             pltpu.SemaphoreType.DMA((N_SEM,)),
             pltpu.SemaphoreType.DMA((N_SEM,)),
@@ -684,9 +699,8 @@
     dq, dk, dv, wg, tg = pl.pallas_call(
         carry,
         out_shape=shapes,
-        in_specs=[anywhere] * 5,
-        out_specs=(anywhere,) * 5,
-        scratch_shapes=[pltpu.SemaphoreType.DMA((5,))],
+        in_specs=[inside] * 5,
+        out_specs=(inside,) * 5,
     )(*made)
     return dq, dk, dv, wg, tg.T
 

time: 142 us -> 82.9 us (0.58)
  Pallas kernels: 140 us -> 80.8 us
    pallas_call x1, Pallas kernels: 52.9 us -> 2.62 us  [on_device(): pl.pallas_call(carry, out_shape=shapes, in_specs=[inside] * 5, out_specs=...]
    pallas_call x1, Pallas kernels: 86.8 us -> 78.2 us  [on_device(): pl.pallas_call(kernel, out_shape=shapes, in_specs=[anywhere] * 6 + [insid...]
where the time goes in v3:
time: 82.9 us; the launch traced here: 82.8 us
  Pallas kernels  80.8 us (97%)
  local copies, waits for them, and re-layouts  1.33 us (2%)
    pallas_call x1, Pallas kernels, on_device(): pl.pallas_call(kernel, out_shape=shapes, in_specs=[anywhere] * 6 + [insid...  78.2 us
    pallas_call x1, Pallas kernels, on_device(): pl.pallas_call(carry, out_shape=shapes, in_specs=[inside] * 5, out_specs=...  2.62 us

profile of v3, /device:TPU:16, one launch (start us, length us, event | category | flops | bytes accessed | tf_op | source)
XLA Modules:
  0.0 82.8 jit_solution(9421297766143894467)
XLA Ops:
  0.6 0.0 copy-start
  0.6 0.7 copy-done
  1.3 0.1 pad.4
  1.4 0.6 broadcast_in_dim.6.bucket_ref
  2.0 78.2 %shard_map.128 = (bf16[512,512]{1,0:T(8,128)(2,1)}, bf16[512,512]{1,0:T(8,128)(2,1)}, bf16[512,512]{1,0:T(8,128)(2,1)}, f32[64,512]{1,0:T(8,128)}, f32[8,32]{1,0:T(8,128)}) custom-call(bf16[512,512]{1,0:T(8,128)(2,1)} %q_hbm.1, bf16[512,512]{1,0:T(8,128)(2,1)} %k_hbm.1, bf16[512,512]{1,0:T(8,128)(2,1)} %v_hbm.1, bf16[512,512]{1,0:T(8,128)(2,1)} %att_hbm.1, ...), custom_call_target="tpu_custom_call" | custom-call | tf_op jit(solution)/shard_map/pallas_call | solution.py:668
  80.1 2.6 %shard_map.129 = (bf16[512,512]{1,0:T(8,128)(2,1)}, bf16[512,512]{1,0:T(8,128)(2,1)}, bf16[512,512]{1,0:T(8,128)(2,1)}, f32[64,512]{1,0:T(8,128)}, f32[8,32]{1,0:T(8,128)}) custom-call(bf16[512,512]{1,0:T(8,128)(2,1)} %get-tuple-element.15.refs_0_, bf16[512,512]{1,0:T(8,128)(2,1)} %get-tuple-element.16.refs_1_, bf16[512,512]{1,0:T(8,128)(2,1)} %get-tuple-element.17.refs_2_, ...), custom_call_target="tpu_custom_call" | custom-call | tf_op jit(solution)/shard_map/pallas_call | solution.py:699
Async XLA Ops:
  0.6 0.7 copy-start

commit v4 on v3

--- a/solution.py
+++ b/solution.py
@@ -246,8 +246,9 @@
         same = seg == spot.astype(F32)
         qaug_ref[...] = jnp.where(same, 1.0, 0.0).astype(BF16)
         kaug_ref[...] = jnp.where((spot < 3) & jnp.logical_not(same), FAR, 0.0).astype(BF16)
-        oh_ref[...] = jnp.where(
-            lax.broadcasted_iota(jnp.int32, (32, WIDE), 0) == bucket_ref[...], 1.0, 0.0
+        oh_ref[...] = jnp.zeros_like(oh_ref)
+        oh_ref[:, BLOCK + 1 : BLOCK + 512] = jnp.where(
+            lax.broadcasted_iota(jnp.int32, (32, 511), 0) == bucket_ref[...], 1.0, 0.0
         )
         bext_ref[...] = jnp.dot(
             table_ref[...], oh_ref[...], precision=lax.Precision.HIGHEST, preferred_element_type=F32
@@ -544,39 +545,39 @@
     gather_b_step(2)
 
     up_end(0)
-    sums_start(0)
     up_hand_on(3)
     up_share(1)
+    sums_start(0)
     gather_b_across(1)
     gather_b_across(7)
     softmax_head(2)
     up_end(1)
-    sums_start(1)
     up_hand_on(4)
     up_share(2)
+    sums_start(1)
     gather_a_step(1)
     softmax_head(3)
     up_end(2)
-    sums_start(2)
     up_hand_on(5)
     up_share(3)
+    sums_start(2)
     gather_b_step(3)
     gather_b_across(2)
     gather_b_across(6)
     softmax_head(4)
     up_end(3)
-    sums_start(3)
     up_hand_on(6)
     up_share(4)
+    sums_start(3)
     sum_a_hop(3, 1, 0)
     sum_a_hop(3, -1, 1)
     sum_c_hop(4, 1)
     gather_a_step(2)
     softmax_head(5)
     up_end(4)
-    sums_start(4)
     up_hand_on(7)
     up_share(5)
+    sums_start(4)
     gather_b_step(4)
     gather_b_across(3)
     gather_b_across(5)
@@ -584,15 +585,15 @@
     sum_b_second(3, 3)
     softmax_head(6)
     up_end(5)
+    up_share(6)
     sums_start(5)
-    up_share(6)
     sum_a_step(2)
     sum_c_step(3)
     gather_a_step(3)
     softmax_head(7)
     up_end(6)
+    up_share(7)
     sums_start(6)
-    up_share(7)
     gather_b_across(4)
     sum_b_second(5, 1)
     sum_b_second(2, 3)
@@ -602,47 +603,47 @@
     sums_start(7)
     sum_a_step(1)
     sum_c_step(2)
-    sum_b_second(6, 1)
-    sum_b_second(1, 3)
     gather_a_end()
     context(0, 0)
     context(0, 1)
     gather_b_end()
+    sum_b_second(6, 1)
+    sum_b_second(1, 3)
     context(1, 0)
     context(1, 1)
     backward_head(0)
     sum_b_second(7, 1)
     sum_b_second(0, 3)
+    sum_b_y(5)
+    sum_b_y(2)
     backward_head(1)
     sum_c_step(1)
-    backward_head(2)
-    sum_b_y(5)
-    sum_b_y(2)
     sum_b_z(4)
     sum_b_z(3)
+    backward_head(2)
+    sum_b_y(6)
+    sum_b_y(1)
     backward_head(3)
     sum_a_x(0)
     sum_a_x(1)
+    sum_b_y(7)
+    sum_b_y(0)
     backward_head(4)
-    sum_b_y(6)
-    sum_b_y(1)
     sum_b_z(5)
     sum_b_z(2)
+    sum_c_x()
     backward_head(5)
-    sum_c_x()
+    sum_b_z(6)
+    sum_b_z(1)
+    backward_head(6)
     sum_a_y()
-    backward_head(6)
-    sum_b_y(7)
-    sum_b_y(0)
+    sum_b_z(7)
+    sum_b_z(0)
     backward_head(7)
     table_z()
-    sum_b_z(6)
-    sum_b_z(1)
-    sum_b_z(7)
-    sum_b_z(0)
     sum_c_end()
+    sum_a_end()
     table_xy()
-    sum_a_end()
     sum_b_end()
     table_end()
     wire.finish()
@@ -654,7 +655,6 @@
 
 
 def on_device(queries, keys, values, attended, upstream, out_weight, bias_table, buckets, segments):
-    shifted = jnp.pad(buckets, (129, WIDE - 129 - buckets.shape[0]), constant_values=-1)[None, :]
     anywhere = pl.BlockSpec(memory_space=pl.ANY)
     inside = pl.BlockSpec(memory_space=pltpu.VMEM)
     bf, f4 = (lambda *s: pltpu.VMEM(s, BF16)), (lambda *s: pltpu.VMEM(s, F32))
@@ -694,7 +694,7 @@
             collective_id=0, has_side_effects=True, vmem_limit_bytes=60 * 1024 * 1024
         ),
     )(
-        queries, keys, values, attended, upstream, out_weight.T, bias_table.T, shifted, segments[None, :]
+        queries, keys, values, attended, upstream, out_weight.T, bias_table.T, buckets[None, :], segments[None, :]
     )
     dq, dk, dv, wg, tg = pl.pallas_call(
         carry,

time: 82.9 us -> 81.8 us (0.987)
  local copies, waits for them, and re-layouts: 1.33 us -> 0 us
where the time goes in v4:
time: 81.8 us; the launch traced here: 81.1 us
  Pallas kernels  80.4 us (98%)
    pallas_call x1, Pallas kernels, on_device(): pl.pallas_call(kernel, out_shape=shapes, in_specs=[anywhere] * 6 + [insid...  77.8 us
    pallas_call x1, Pallas kernels, on_device(): pl.pallas_call(carry, out_shape=shapes, in_specs=[inside] * 5, out_specs=...  2.62 us

profile of v4, /device:TPU:16, one launch (start us, length us, event | category | flops | bytes accessed | tf_op | source)
XLA Modules:
  0.0 81.1 jit_solution(15739802387170061500)
XLA Ops:
  0.6 77.8 %shard_map.128 = (bf16[512,512]{1,0:T(8,128)(2,1)}, bf16[512,512]{1,0:T(8,128)(2,1)}, bf16[512,512]{1,0:T(8,128)(2,1)}, f32[64,512]{1,0:T(8,128)}, f32[8,32]{1,0:T(8,128)}) custom-call(bf16[512,512]{1,0:T(8,128)(2,1)} %q_hbm.1, bf16[512,512]{1,0:T(8,128)(2,1)} %k_hbm.1, bf16[512,512]{1,0:T(8,128)(2,1)} %v_hbm.1, bf16[512,512]{1,0:T(8,128)(2,1)} %att_hbm.1, ...), custom_call_target="tpu_custom_call" | custom-call | tf_op jit(solution)/shard_map/pallas_call | solution.py:668
  78.5 2.6 %shard_map.129 = (bf16[512,512]{1,0:T(8,128)(2,1)}, bf16[512,512]{1,0:T(8,128)(2,1)}, bf16[512,512]{1,0:T(8,128)(2,1)}, f32[64,512]{1,0:T(8,128)}, f32[8,32]{1,0:T(8,128)}) custom-call(bf16[512,512]{1,0:T(8,128)(2,1)} %get-tuple-element.15.refs_0_, bf16[512,512]{1,0:T(8,128)(2,1)} %get-tuple-element.16.refs_1_, bf16[512,512]{1,0:T(8,128)(2,1)} %get-tuple-element.17.refs_2_, ...), custom_call_target="tpu_custom_call" | custom-call | tf_op jit(solution)/shard_map/pallas_call | solution.py:699
